TPU v7x, 256 devices: a whole 4x4x8 slice. The times are simulated.
256 devices in a mesh: member: 8 (over x, y_hi), tile: 32 (over z, y_lo, core).
Axes of the slice: x: 4, y: 4 (y_hi: 2, y_lo: 2; y = y_hi * 2 + y_lo), z: 8, core: 2. Of those that a mesh axis runs over, the one named last changes fastest.
Arguments:
- precip: float32 [4096, 256], P(('member', 'tile')), parts along dimension 0, may hold values from 0.2 to 2
- pet: float32 [4096, 256], P(('member', 'tile')), parts along dimension 0, may hold values from 0.05 to 0.5
- soil_init: float32 [4096, 256], P(('member', 'tile')), parts along dimension 0, may hold values from 0.05 to 0.4
- ksat: float32 [4096, 256], P(('member', 'tile')), parts along dimension 0, may hold values from 0.5 to 3
- land_mask: int32 [4096, 256], P(('member', 'tile')), parts along dimension 0, may hold values 0 or 1
- head_init: float32 [8192, 2048], P(('member', 'tile')), parts along dimension 0, may hold values from 0.2 to 2
- subsurface_init: float32 [8192, 2048], P(('member', 'tile')), parts along dimension 0, may hold values from 0.2 to 2
- conduct: float32 [8192, 2048], P(('member', 'tile')), parts along dimension 0, may hold values from 0.22 to 0.47
- drain_rate: float32 [8192, 2048], P(('member', 'tile')), parts along dimension 0, may hold values from 0.05 to 0.4
- flow_code: int32 [8192, 2048], P(('member', 'tile')), parts along dimension 0, may hold values from 0 to 3
- channel_share: float32 [8192, 2048], P(('member', 'tile')), parts along dimension 0, may hold values from 0.02 to 0.2
- cell_slot: int32 [8192, 2048], P(('member', 'tile')), parts along dimension 0, may hold values from 0 to 2047
- slot_reach: int32 [524288], P(('member', 'tile')), parts along dimension 0, may hold values from 0 to 2047
Outputs:
- soil: float32 [4096, 256], P(('member', 'tile')), parts along dimension 0
- head: float32 [8192, 2048], P(('member', 'tile')), parts along dimension 0
- subsurface: float32 [8192, 2048], P(('member', 'tile')), parts along dimension 0
- reach_inflow: float32 [524288], P(('member', 'tile')), parts along dimension 0
There are 8 independent parts, one for each index of `member`. A program takes and returns all parts, laid end to end along the dimension named above; each array names one. Nothing has to cross between parts.
Inputs may be any that keep to these rules, and one draw needn't show every extreme that they name: `slot_reach`: slot k of a tile holds a reach owned by tile index k // 64.
All inputs are finite; a program needn't handle non-finite values. No bound on the sum of `land_mask` on one device may be relied on, other than what follows from the above.
Results may differ from a plain program's by a relative error of at most 0.00002.
Values sent between devices are 32-bit elements; how exact they have to be, the bound alone decides.
No kernel may reach another device: no remote copies, remote signals or barrier semaphores. Data moves between devices by JAX's collectives and lax.ppermute only.
A program may use at most 64 MiB of HBM per device.

v0:
```python
import jax
import jax.numpy as jnp
from jax import lax
from jax.sharding import PartitionSpec as P

ITERS = 6


def padded(x, sides, width):
    for axis, dim in sides:
        peers, length = (lax.axis_size(axis), x.shape[dim])
        up = [(i, (i + 1) % peers) for i in range(peers - 1)]
        down = [(j, i) for i, j in up]
        last = lax.slice_in_dim(x, length - width, length, axis=dim)
        first = lax.slice_in_dim(x, 0, width, axis=dim)
        before = lax.ppermute(last, axis, up)
        after = lax.ppermute(first, axis, down)
        x = jnp.concatenate([before, x, after], axis=dim)
    return x


def land_step(precip, pet, soil_init, ksat, land_mask):
    mask = land_mask.astype(jnp.float32)
    wet = 2.0 * soil_init
    cap = ksat * (1.0 - wet)
    runoff = mask * precip * precip / (precip + cap)
    drainage = 0.25 * mask * ksat * wet**4
    evap = mask * pet * wet
    soil = soil_init + 0.1 * (mask * precip - runoff - drainage - evap)
    return (soil, runoff, drainage)


def advance(state, statics):
    h = state[0]
    s = state[1]
    g, down, up, right, left = (statics[0], statics[1], statics[2], statics[3], statics[4])
    hc = h[1:-1]
    gc = g[1:-1]
    sc = s[1:-1]
    hs = jnp.pad(hc, ((0, 0), (1, 1)))
    gs = jnp.pad(gc, ((0, 0), (1, 1)))
    flux = g[:-2] * (h[:-2] - hc) + g[2:] * (h[2:] - hc)
    flux = flux + gs[:, :-2] * (hs[:, :-2] - hc) + gs[:, 2:] * (hs[:, 2:] - hc)
    h_new = hc + gc * flux
    moving_right = jnp.pad((right * s)[1:-1], ((0, 0), (1, 1)))
    moving_left = jnp.pad((left * s)[1:-1], ((0, 0), (1, 1)))
    incoming = (down * s)[:-2] + (up * s)[2:] + moving_right[:, :-2] + moving_left[:, 2:]
    outgoing = (down + up + right + left)[1:-1]
    s_new = sc - outgoing * sc + incoming
    return jnp.stack([h_new, s_new])


def slot_totals(inflow, cell_slot, slots):
    slot_line = lax.broadcasted_iota(jnp.int32, (1, slots), 1)

    def add_block(total, pair):
        block_values, block_labels = pair
        hit = block_labels[:, None] == slot_line
        return (total + jnp.sum(jnp.where(hit, block_values[:, None], 0.0), axis=0), None)

    total, unused = lax.scan(add_block, jnp.zeros((slots,), jnp.float32), (inflow, cell_slot))
    return total


def spread_reaches(sums, places, reach_dev):
    reach_line = lax.broadcasted_iota(jnp.int32, (1, 1, reach_dev), 2)
    hit = places[:, :, None] == reach_line
    return jnp.sum(jnp.where(hit, sums[:, :, None], 0.0), axis=1)


def local(
    precip,
    pet,
    soil_init,
    ksat,
    land_mask,
    head_init,
    subsurface_init,
    conduct,
    drain_rate,
    flow_code,
    channel_share,
    cell_slot,
    slot_reach,
):
    soil, runoff, drainage = land_step(precip, pet, soil_init, ksat, land_mask)
    moved = lax.all_to_all(
        jnp.stack([runoff, drainage]), "tile", split_axis=2, concat_axis=1, tiled=True
    )
    fine = jnp.swapaxes(moved, 1, 2)
    fine = jnp.repeat(jnp.repeat(fine, 4, axis=1), 4, axis=2)
    state = jnp.stack([head_init + fine[0], subsurface_init + fine[1]])
    margin = 1
    parts = [conduct]
    for code in range(4):
        parts.append(drain_rate * (flow_code == code).astype(jnp.float32))
    statics = jnp.stack(parts)
    padded_static = padded(statics, (("tile", 1),), margin)
    for step in range(ITERS):
        widened = padded(state, (("tile", 1),), 1)
        state = advance(widened, padded_static)
    h = state[0]
    inflow = channel_share * h
    head = h - inflow
    tiles = lax.axis_size("tile")
    slots = slot_reach.shape[0]
    per_owner = slots // tiles
    slot_sums = slot_totals(inflow, cell_slot, slots)
    partial_sums = spread_reaches(
        slot_sums.reshape(tiles, per_owner), slot_reach.reshape(tiles, per_owner), slots
    ).reshape(tiles * slots)
    reach_inflow = lax.psum_scatter(partial_sums, "tile", scatter_dimension=0, tiled=True)
    return (soil, head, state[1], reach_inflow)


def solution(mesh):
    placed = (
        P(("member", "tile"), None),
        P(("member", "tile"), None),
        P(("member", "tile"), None),
        P(("member", "tile"), None),
        P(("member", "tile"), None),
        P(("member", "tile"), None),
        P(("member", "tile"), None),
        P(("member", "tile"), None),
        P(("member", "tile"), None),
        P(("member", "tile"), None),
        P(("member", "tile"), None),
        P(("member", "tile"), None),
        P(("member", "tile")),
    )
    return jax.shard_map(
        local,
        mesh=mesh,
        in_specs=placed,
        out_specs=(
            P(("member", "tile"), None),
            P(("member", "tile"), None),
            P(("member", "tile"), None),
            P(("member", "tile")),
        ),
        check_vma=False,
    )
```

profile of v0, /device:TPU:1, one launch (start us, length us, event | category | flops | bytes accessed | tf_op | source)
XLA Modules:
  0.0 563.5 jit_solution(14176274257659304468)
XLA Ops:
  10.6 4.7 collective-permute-start
  19.1 11.3 %all-to-all-start = ((f32[32,1,256]{2,1,0:T(1,128)}), f32[32,1,256]{2,1,0:T(1,128)S(1)}, u32[]{:S(2)}, u32[]{:S(2)}) async-start(f32[32,1,256]{2,1,0:T(1,128)} %reshape.77), calls=%async_computation | async-start | bytes 65536 | tf_op jit(solution)/shard_map/all_to_all | solution.py:87
  34.8 3.7 all-to-all-done
  46.7 2.3 collective-permute-start.3
  49.6 3.7 collective-permute-start.1
  64.6 2.6 fusion.86
  68.6 2.3 fusion.96
  73.2 2.7 fusion.4
  75.8 2.7 slice_maximum_fusion.4
  82.7 2.2 copy.268
  84.9 4.2 collective-permute-start.4
  93.0 6.3 %fusion.81 = f32[32,2048]{0,1:T(8,128)S(1)} fusion(f32[32,2048]{0,1:T(8,128)} %copy-done.31, f32[32,2048]{0,1:T(8,128)} %copy.261, f32[2,1,2048]{1,2,0:T(8,128)} %copy.271, f32[1,32,2048]{1,2,0:T(8,128)} %bitcast.255, f32[1,32,2048]{1,2,0:T(8,128)} %bitcast.276, f32[2,1,2048]{1,2,0:T(8,128)} %copy.269, f32[1,32,2048]{1,2,0:T(8,128)} %copy.308, ...), kind=kLoop, calls=%fused_computation.159 | loop fusion | flops 1114112 | bytes 1867776 | tf_op jit(solution)/shard_map/add | solution.py:44
  102.4 2.7 slice_maximum_fusion.3
  111.4 3.6 collective-permute-start.6
  119.1 6.2 %fusion.68 = f32[32,2048]{0,1:T(8,128)S(1)} fusion(f32[32,2048]{0,1:T(8,128)} %copy-done.33, f32[32,2048]{0,1:T(8,128)} %copy.261, f32[2,1,2048]{1,2,0:T(8,128)} %copy.278, f32[1,32,2048]{1,2,0:T(8,128)} %bitcast.261, f32[1,32,2048]{1,2,0:T(8,128)} %bitcast.279, f32[2,1,2048]{1,2,0:T(8,128)} %copy.276, f32[1,32,2048]{1,2,0:T(8,128)} %copy.308, ...), kind=kLoop, calls=%fused_computation.137 | loop fusion | flops 1114112 | bytes 1867776 | tf_op jit(solution)/shard_map/add | solution.py:44
  128.4 2.7 slice_maximum_fusion.2
  137.5 3.8 collective-permute-start.8
  145.3 6.2 %fusion.55 = f32[32,2048]{0,1:T(8,128)S(1)} fusion(f32[32,2048]{0,1:T(8,128)} %copy-done.35, f32[32,2048]{0,1:T(8,128)} %copy.261, f32[2,1,2048]{1,2,0:T(8,128)} %copy.285, f32[1,32,2048]{1,2,0:T(8,128)} %bitcast.264, f32[1,32,2048]{1,2,0:T(8,128)} %bitcast.282, f32[2,1,2048]{1,2,0:T(8,128)} %copy.283, f32[1,32,2048]{1,2,0:T(8,128)} %copy.308, ...), kind=kLoop, calls=%fused_computation.115 | loop fusion | flops 1114112 | bytes 1867776 | tf_op jit(solution)/shard_map/add | solution.py:44
  154.6 2.7 slice_maximum_fusion.1
  163.7 3.6 collective-permute-start.10
  171.3 6.2 %fusion.42 = f32[32,2048]{0,1:T(8,128)S(1)} fusion(f32[32,2048]{0,1:T(8,128)} %copy-done.37, f32[32,2048]{0,1:T(8,128)} %copy.261, f32[2,1,2048]{1,2,0:T(8,128)} %copy.292, f32[1,32,2048]{1,2,0:T(8,128)} %bitcast.267, f32[1,32,2048]{1,2,0:T(8,128)} %bitcast.285, f32[2,1,2048]{1,2,0:T(8,128)} %copy.290, f32[1,32,2048]{1,2,0:T(8,128)} %copy.308, ...), kind=kLoop, calls=%fused_computation.93 | loop fusion | flops 1114112 | bytes 1867776 | tf_op jit(solution)/shard_map/add | solution.py:44
  180.7 2.7 slice_maximum_fusion
  183.4 2.3 copy.298
  189.9 4.7 collective-permute-start.12
  201.3 2.6 fusion.21
  205.4 4.5 fusion.102
  213.8 107.4 %while.11 = (s32[]{:T(128)}, f32[2048]{0:T(1024)S(1)}, s32[32,2048]{1,0:T(8,128)}, f32[32,2048]{1,0:T(8,128)S(1)}, s32[]{:T(128)}, /*index=5*/s32[]{:T(128)}) while((s32[]{:T(128)}, f32[2048]{0:T(1024)S(1)}, s32[32,2048]{1,0:T(8,128)}, f32[32,2048]{1,0:T(8,128)S(1)}, s32[]{:T(128)}, /*index=5*/s32[]{:T(128)}) %tuple.58), condition=%wide.region_2.3_spmd.clone, body=%wide.region_0.2_spmd.clone.sunk | while | flops 12584963 | bytes 82015 | solution.py:61
  214.7 2.4 select_reduce_fusion.3
  218.0 2.4 select_reduce_fusion.3
  221.4 2.4 select_reduce_fusion.3
  224.8 2.4 select_reduce_fusion.3
  228.1 2.4 select_reduce_fusion.3
  231.5 2.4 select_reduce_fusion.3
  234.8 2.4 select_reduce_fusion.3
  238.2 2.4 select_reduce_fusion.3
  241.5 2.4 select_reduce_fusion.3
  244.9 2.4 select_reduce_fusion.3
  248.3 2.4 select_reduce_fusion.3
  251.6 2.4 select_reduce_fusion.3
  255.0 2.4 select_reduce_fusion.3
  258.3 2.4 select_reduce_fusion.3
  261.7 2.4 select_reduce_fusion.3
  265.0 2.4 select_reduce_fusion.3
  268.4 2.4 select_reduce_fusion.3
  271.8 2.4 select_reduce_fusion.3
  275.1 2.4 select_reduce_fusion.3
  278.5 2.4 select_reduce_fusion.3
  281.8 2.4 select_reduce_fusion.3
  285.2 2.4 select_reduce_fusion.3
  288.5 2.4 select_reduce_fusion.3
  291.9 2.4 select_reduce_fusion.3
  295.3 2.4 select_reduce_fusion.3
  298.6 2.4 select_reduce_fusion.3
  302.0 2.4 select_reduce_fusion.3
  305.3 2.4 select_reduce_fusion.3
  308.7 2.4 select_reduce_fusion.3
  312.0 2.4 select_reduce_fusion.3
  315.4 2.4 select_reduce_fusion.3
  318.8 2.4 select_reduce_fusion.3
  321.3 3.0 select_reduce_fusion.1
  325.1 4.1 fusion.19
  329.2 2.2 copy.305
  331.5 2.2 copy.306
  333.7 221.5 %all-reduce.22.cloned.1.call-done = f32[65536]{0:T(1024)} async-done(((f32[65536]{0:T(1024)}), f32[65536]{0:T(1024)}) %all-reduce.22.cloned.1.call-update) | async-done | bytes 262160
  (349 shorter events, 131.6 us)
Async XLA Ops:
  7.2 3.3 copy-start.57
  7.2 3.3 copy-start.58
  7.2 10.1 %copy-start.67 = (f32[16,256]{1,0:T(8,128)S(1)}, f32[16,256]{1,0:T(8,128)}, u32[]{:S(2)}) copy-start(f32[16,256]{1,0:T(8,128)} %param.15) | copy-start | bytes 49156
  7.2 10.1 %copy-start.68 = (f32[16,256]{1,0:T(8,128)S(1)}, f32[16,256]{1,0:T(8,128)}, u32[]{:S(2)}) copy-start(f32[16,256]{1,0:T(8,128)} %param.18) | copy-start | bytes 49156
  7.2 10.1 %copy-start.69 = (f32[16,256]{1,0:T(8,128)S(1)}, f32[16,256]{1,0:T(8,128)}, u32[]{:S(2)}) copy-start(f32[16,256]{1,0:T(8,128)} %param.17) | copy-start | bytes 49156
  7.2 10.1 %copy-start.70 = (s32[16,256]{1,0:T(8,128)S(1)}, s32[16,256]{1,0:T(8,128)}, u32[]{:S(2)}) copy-start(s32[16,256]{1,0:T(8,128)} %param.19) | copy-start | bytes 49156
  7.2 10.1 %copy-start.71 = (f32[16,256]{1,0:T(8,128)S(1)}, f32[16,256]{1,0:T(8,128)}, u32[]{:S(2)}) copy-start(f32[16,256]{1,0:T(8,128)} %param.16) | copy-start | bytes 49156
  8.3 22.2 %copy-start.63 = (f32[32,2048]{1,0:T(8,128)S(1)}, f32[32,2048]{1,0:T(8,128)}, u32[]{:S(2)}) copy-start(f32[32,2048]{1,0:T(8,128)} %param.22) | copy-start | bytes 786436
  10.5 21.3 %copy-start.64 = (f32[32,2048]{1,0:T(8,128)S(1)}, f32[32,2048]{1,0:T(8,128)}, u32[]{:S(2)}) copy-start(f32[32,2048]{1,0:T(8,128)} %param.20) | copy-start | bytes 786436
  10.6 22.9 %copy-start.56 = (f32[5,32,2048]{2,1,0:T(8,128)}, f32[5,32,2048]{2,1,0:T(8,128)S(1)}, u32[]{:S(2)}) copy-start(f32[5,32,2048]{2,1,0:T(8,128)S(1)} %bitcast_dynamic-update-slice_fusion) | copy-start | bytes 3932164
  10.6 22.5 %copy-start.65 = (f32[32,2048]{1,0:T(8,128)S(1)}, f32[32,2048]{1,0:T(8,128)}, u32[]{:S(2)}) copy-start(f32[32,2048]{1,0:T(8,128)} %param.21) | copy-start | bytes 786436
  10.6 22.8 %collective-permute-start = (f32[5,1,2048]{2,1,0:T(1,128)S(1)}, f32[5,1,2048]{2,1,0:T(1,128)S(1)}, u32[]{:S(2)}, u32[]{:S(2)}) collective-permute-start(f32[5,1,2048]{2,1,0:T(1,128)S(1)} %get-tuple-element.119), channel_id=1, source_target_pairs={{0,1},{1,2},{2,3},{3,4},{4,5},{5,6},{6,7},{7,8},{8,9},{9,10},{10,1... | collective-permute-start | bytes 122888 | tf_op jit(solution)/shard_map/ppermute | solution.py:16
  15.4 18.1 %collective-permute-start.2 = (f32[5,1,2048]{2,1,0:T(1,128)S(1)}, f32[5,1,2048]{2,1,0:T(1,128)S(1)}, u32[]{:S(2)}, u32[]{:S(2)}) collective-permute-start(f32[5,1,2048]{2,1,0:T(1,128)S(1)} %get-tuple-element.120), channel_id=1, source_target_pairs={{1,0},{2,1},{3,2},{4,3},{5,4},{6,5},{7,6},{8,7},{9,8},{10,9},{11,1... | collective-permute-start | bytes 122888 | tf_op jit(solution)/shard_map/ppermute | solution.py:17
  19.1 19.4 %all-to-all-start = ((f32[32,1,256]{2,1,0:T(1,128)}), f32[32,1,256]{2,1,0:T(1,128)S(1)}, u32[]{:S(2)}, u32[]{:S(2)}) async-start(f32[32,1,256]{2,1,0:T(1,128)} %reshape.77), calls=%async_computation | async-start | bytes 65536 | tf_op jit(solution)/shard_map/all_to_all | solution.py:87
  30.4 524.8 %all-reduce.22.cloned.1.call-start = ((), (), s32[]{:S(2)}) async-start(), calls=%async_computation.1 | async-start | bytes 524288
  33.4 7.9 %copy-start.52 = (f32[32,2048]{0,1:T(8,128)}, f32[32,2048]{0,1:T(8,128)S(1)}, u32[]{:S(2)}) copy-start(f32[32,2048]{0,1:T(8,128)S(1)} %copy.254) | copy-start | bytes 786436
  34.8 6.2 %copy-start.59 = (f32[32,2048]{0,1:T(8,128)S(1)}, f32[32,2048]{0,1:T(8,128)}, u32[]{:S(2)}) copy-start(f32[32,2048]{0,1:T(8,128)} %copy.251) | copy-start | bytes 786436
  46.7 13.9 %collective-permute-start.3 = (f32[2,1,2048]{2,0,1:T(2,128)S(1)}, f32[2,1,2048]{2,0,1:T(2,128)S(1)}, u32[]{:S(2)}, u32[]{:S(2)}) collective-permute-start(f32[2,1,2048]{2,0,1:T(2,128)S(1)} %copy.258), channel_id=1, source_target_pairs={{1,0},{2,1},{3,2},{4,3},{5,4},{6,5},{7,6},{8,7},{9,8},{10,9},{11,1... | collective-permute-start | bytes 49160 | tf_op jit(solution)/shard_map/ppermute | solution.py:17
  49.6 7.6 %copy-start.62 = (f32[1,34,2048]{2,1,0:T(8,128)S(1)}, f32[1,34,2048]{2,1,0:T(8,128)}, u32[]{:S(2)}) copy-start(f32[1,34,2048]{2,1,0:T(8,128)} %get-tuple-element.116) | copy-start | bytes 835588
  49.6 13.0 %collective-permute-start.1 = (f32[2,1,2048]{2,0,1:T(2,128)S(1)}, f32[2,1,2048]{2,0,1:T(2,128)S(1)}, u32[]{:S(2)}, u32[]{:S(2)}) collective-permute-start(f32[2,1,2048]{2,0,1:T(2,128)S(1)} %copy.255), channel_id=1, source_target_pairs={{0,1},{1,2},{2,3},{3,4},{4,5},{5,6},{6,7},{7,8},{8,9},{9,10},{10,1... | collective-permute-start | bytes 49160 | tf_op jit(solution)/shard_map/ppermute | solution.py:16
  54.4 3.2 copy-start.61
  64.5 3.1 copy-start.28
  64.5 3.8 copy-start.40
  64.6 4.0 copy-start.51
  70.9 4.9 copy-start.31
  80.7 8.3 %collective-permute-start.5 = (f32[2,1,2048]{2,0,1:T(2,128)S(1)}, f32[2,1,2048]{2,0,1:T(2,128)S(1)}, u32[]{:S(2)}, u32[]{:S(2)}) collective-permute-start(f32[2,1,2048]{2,0,1:T(2,128)S(1)} %copy.270), channel_id=1, source_target_pairs={{1,0},{2,1},{3,2},{4,3},{5,4},{6,5},{7,6},{8,7},{9,8},{10,9},{11,1... | collective-permute-start | bytes 49160 | tf_op jit(solution)/shard_map/ppermute | solution.py:17
  84.9 6.2 %collective-permute-start.4 = (f32[2,1,2048]{2,0,1:T(2,128)S(1)}, f32[2,1,2048]{2,0,1:T(2,128)S(1)}, u32[]{:S(2)}, u32[]{:S(2)}) collective-permute-start(f32[2,1,2048]{2,0,1:T(2,128)S(1)} %copy.268), channel_id=1, source_target_pairs={{0,1},{1,2},{2,3},{3,4},{4,5},{5,6},{6,7},{7,8},{8,9},{9,10},{10,1... | collective-permute-start | bytes 49160 | tf_op jit(solution)/shard_map/ppermute | solution.py:16
  93.0 6.3 %copy-start.18 = (f32[32,2048]{0,1:T(8,128)S(1)}, f32[32,2048]{0,1:T(8,128)}, u32[]{:S(2)}) copy-start(f32[32,2048]{0,1:T(8,128)} %copy-done.17) | copy-start | bytes 786436
  93.0 6.3 %copy-start.32 = (f32[32,2048]{0,1:T(8,128)S(1)}, f32[32,2048]{0,1:T(8,128)}, u32[]{:S(2)}) copy-start(f32[32,2048]{0,1:T(8,128)} %copy-done.31) | copy-start | bytes 786436
  93.0 6.3 %copy-start.41 = (f32[2,1,2048]{1,2,0:T(8,128)S(1)}, f32[2,1,2048]{1,2,0:T(8,128)}, u32[]{:S(2)}) copy-start(f32[2,1,2048]{1,2,0:T(8,128)} %copy.271) | copy-start | bytes 49156
  93.0 6.5 %copy-start.45 = (f32[2,1,2048]{1,2,0:T(8,128)S(1)}, f32[2,1,2048]{1,2,0:T(8,128)}, u32[]{:S(2)}) copy-start(f32[2,1,2048]{1,2,0:T(8,128)} %copy.269) | copy-start | bytes 49156
  99.5 2.8 copy-start.33
  107.3 7.8 %collective-permute-start.7 = (f32[2,1,2048]{2,0,1:T(2,128)S(1)}, f32[2,1,2048]{2,0,1:T(2,128)S(1)}, u32[]{:S(2)}, u32[]{:S(2)}) collective-permute-start(f32[2,1,2048]{2,0,1:T(2,128)S(1)} %copy.277), channel_id=1, source_target_pairs={{1,0},{2,1},{3,2},{4,3},{5,4},{6,5},{7,6},{8,7},{9,8},{10,9},{11,1... | collective-permute-start | bytes 49160 | tf_op jit(solution)/shard_map/ppermute | solution.py:17
  111.4 5.6 collective-permute-start.6
  119.0 6.2 %copy-start.22 = (f32[32,2048]{0,1:T(8,128)S(1)}, f32[32,2048]{0,1:T(8,128)}, u32[]{:S(2)}) copy-start(f32[32,2048]{0,1:T(8,128)} %copy-done.21) | copy-start | bytes 786436
  119.0 6.2 %copy-start.34 = (f32[32,2048]{0,1:T(8,128)S(1)}, f32[32,2048]{0,1:T(8,128)}, u32[]{:S(2)}) copy-start(f32[32,2048]{0,1:T(8,128)} %copy-done.33) | copy-start | bytes 786436
  119.1 6.3 %copy-start.42 = (f32[2,1,2048]{1,2,0:T(8,128)S(1)}, f32[2,1,2048]{1,2,0:T(8,128)}, u32[]{:S(2)}) copy-start(f32[2,1,2048]{1,2,0:T(8,128)} %copy.278) | copy-start | bytes 49156
  119.1 6.5 %copy-start.46 = (f32[2,1,2048]{1,2,0:T(8,128)S(1)}, f32[2,1,2048]{1,2,0:T(8,128)}, u32[]{:S(2)}) copy-start(f32[2,1,2048]{1,2,0:T(8,128)} %copy.276) | copy-start | bytes 49156
  125.6 2.8 copy-start.35
  133.3 8.0 %collective-permute-start.9 = (f32[2,1,2048]{2,0,1:T(2,128)S(1)}, f32[2,1,2048]{2,0,1:T(2,128)S(1)}, u32[]{:S(2)}, u32[]{:S(2)}) collective-permute-start(f32[2,1,2048]{2,0,1:T(2,128)S(1)} %copy.284), channel_id=1, source_target_pairs={{1,0},{2,1},{3,2},{4,3},{5,4},{6,5},{7,6},{8,7},{9,8},{10,9},{11,1... | collective-permute-start | bytes 49160 | tf_op jit(solution)/shard_map/ppermute | solution.py:17
  137.5 5.8 %collective-permute-start.8 = (f32[2,1,2048]{2,0,1:T(2,128)S(1)}, f32[2,1,2048]{2,0,1:T(2,128)S(1)}, u32[]{:S(2)}, u32[]{:S(2)}) collective-permute-start(f32[2,1,2048]{2,0,1:T(2,128)S(1)} %copy.282), channel_id=1, source_target_pairs={{0,1},{1,2},{2,3},{3,4},{4,5},{5,6},{6,7},{7,8},{8,9},{9,10},{10,1... | collective-permute-start | bytes 49160 | tf_op jit(solution)/shard_map/ppermute | solution.py:16
  145.3 6.2 %copy-start.24 = (f32[32,2048]{0,1:T(8,128)S(1)}, f32[32,2048]{0,1:T(8,128)}, u32[]{:S(2)}) copy-start(f32[32,2048]{0,1:T(8,128)} %copy-done.23) | copy-start | bytes 786436
  145.3 6.2 %copy-start.36 = (f32[32,2048]{0,1:T(8,128)S(1)}, f32[32,2048]{0,1:T(8,128)}, u32[]{:S(2)}) copy-start(f32[32,2048]{0,1:T(8,128)} %copy-done.35) | copy-start | bytes 786436
  145.3 6.3 %copy-start.43 = (f32[2,1,2048]{1,2,0:T(8,128)S(1)}, f32[2,1,2048]{1,2,0:T(8,128)}, u32[]{:S(2)}) copy-start(f32[2,1,2048]{1,2,0:T(8,128)} %copy.285) | copy-start | bytes 49156
  145.3 6.5 %copy-start.47 = (f32[2,1,2048]{1,2,0:T(8,128)S(1)}, f32[2,1,2048]{1,2,0:T(8,128)}, u32[]{:S(2)}) copy-start(f32[2,1,2048]{1,2,0:T(8,128)} %copy.283) | copy-start | bytes 49156
  151.8 2.8 copy-start.37
  159.5 7.8 %collective-permute-start.11 = (f32[2,1,2048]{2,0,1:T(2,128)S(1)}, f32[2,1,2048]{2,0,1:T(2,128)S(1)}, u32[]{:S(2)}, u32[]{:S(2)}) collective-permute-start(f32[2,1,2048]{2,0,1:T(2,128)S(1)} %copy.291), channel_id=1, source_target_pairs={{1,0},{2,1},{3,2},{4,3},{5,4},{6,5},{7,6},{8,7},{9,8},{10,9},{11,1... | collective-permute-start | bytes 49160 | tf_op jit(solution)/shard_map/ppermute | solution.py:17
  163.7 5.6 collective-permute-start.10
  171.3 6.2 %copy-start.26 = (f32[32,2048]{0,1:T(8,128)S(1)}, f32[32,2048]{0,1:T(8,128)}, u32[]{:S(2)}) copy-start(f32[32,2048]{0,1:T(8,128)} %copy-done.25) | copy-start | bytes 786436
  171.3 6.2 %copy-start.38 = (f32[32,2048]{0,1:T(8,128)S(1)}, f32[32,2048]{0,1:T(8,128)}, u32[]{:S(2)}) copy-start(f32[32,2048]{0,1:T(8,128)} %copy-done.37) | copy-start | bytes 786436
  171.3 6.3 %copy-start.44 = (f32[2,1,2048]{1,2,0:T(8,128)S(1)}, f32[2,1,2048]{1,2,0:T(8,128)}, u32[]{:S(2)}) copy-start(f32[2,1,2048]{1,2,0:T(8,128)} %copy.292) | copy-start | bytes 49156
  171.3 6.5 %copy-start.48 = (f32[2,1,2048]{1,2,0:T(8,128)S(1)}, f32[2,1,2048]{1,2,0:T(8,128)}, u32[]{:S(2)}) copy-start(f32[2,1,2048]{1,2,0:T(8,128)} %copy.290) | copy-start | bytes 49156
  177.8 2.8 copy-start.29
  183.4 11.3 %copy-start.66 = (f32[32,2048]{1,0:T(8,128)S(1)}, f32[32,2048]{1,0:T(8,128)}, u32[]{:S(2)}) copy-start(f32[32,2048]{1,0:T(8,128)} %param.25) | copy-start | bytes 786436
  185.6 10.4 %copy-start.72 = (s32[2048]{0:T(1024)S(1)}, s32[2048]{0:T(1024)}, u32[]{:S(2)}) copy-start(s32[2048]{0:T(1024)} %param.27) | copy-start | bytes 24580
  185.6 10.4 %copy-start.73 = (u32[256]{0:T(256)S(1)}, u32[256]{0:T(256)}, u32[]{:S(2)}) copy-start(u32[256]{0:T(256)} %constant.88) | copy-start | bytes 3076
  185.6 11.7 %collective-permute-start.13 = (f32[2,1,2048]{2,0,1:T(2,128)S(1)}, f32[2,1,2048]{2,0,1:T(2,128)S(1)}, u32[]{:S(2)}, u32[]{:S(2)}) collective-permute-start(f32[2,1,2048]{2,0,1:T(2,128)S(1)} %copy.298), channel_id=1, source_target_pairs={{1,0},{2,1},{3,2},{4,3},{5,4},{6,5},{7,6},{8,7},{9,8},{10,9},{11,1... | collective-permute-start | bytes 49160 | tf_op jit(solution)/shard_map/ppermute | solution.py:17
  189.9 9.4 %collective-permute-start.12 = (f32[2,1,2048]{2,0,1:T(2,128)S(1)}, f32[2,1,2048]{2,0,1:T(2,128)S(1)}, u32[]{:S(2)}, u32[]{:S(2)}) collective-permute-start(f32[2,1,2048]{2,0,1:T(2,128)S(1)} %copy.296), channel_id=1, source_target_pairs={{0,1},{1,2},{2,3},{3,4},{4,5},{5,6},{6,7},{7,8},{8,9},{9,10},{10,1... | collective-permute-start | bytes 49160 | tf_op jit(solution)/shard_map/ppermute | solution.py:16
  201.3 3.1 copy-start.20
  201.3 3.4 copy-start.30
  201.3 4.1 copy-start.39
  205.4 4.5 copy-start.49
  212.1 113.0 %copy-start.5 = (f32[1,34,2048]{1,2,0:T(8,128)S(1)}, f32[1,34,2048]{1,2,0:T(8,128)}, u32[]{:S(2)}) copy-start(f32[1,34,2048]{1,2,0:T(8,128)} %copy.309) | copy-start | bytes 835588
  212.1 113.0 %copy-start.16 = (f32[32,2048]{0,1:T(8,128)S(1)}, f32[32,2048]{0,1:T(8,128)}, u32[]{:S(2)}) copy-start(f32[32,2048]{0,1:T(8,128)} %get-tuple-element.100) | copy-start | bytes 786436
  (26 other events, 53.2 us)
Sparse Core Ops, SparseCore 0:
  325.2 229.9 all-reduce.21
where the time goes:
time: 570 us; the launch traced here: 564 us
  waiting for transfers between devices  225 us (39%)
  other arithmetic  158 us (28%)
  local copies, waits for them, and re-layouts  109 us (19%)
  starting transfers between devices  53.7 us (9%)
  between operations  16 us (3%)
    unnamed x2, waiting for transfers between devices  221 us
    reduce_sum x32, other arithmetic, add_block(): jnp.sum(jnp.where(hit, block_values[:, None], 0.0), axis=0)  78.1 us
    unnamed x167, local copies, waits for them, and re-layouts  30.6 us
    ppermute x7, starting transfers between devices, padded(): before = lax.ppermute(last, axis, up)  28.4 us
    dynamic_slice x64, local copies, waits for them, and re-layouts, slot_totals(): lax.scan(add_block, jnp.zeros((slots,), jnp.float32), (inflow, cell_slot))  27.8 us
    add x5, other arithmetic, advance(): h_new = hc + gc * flux  27.3 us
    ppermute x7, starting transfers between devices, padded(): after = lax.ppermute(first, axis, down)  14 us
    another operation x5, other arithmetic, advance(): return jnp.stack([h_new, s_new])  13.4 us
  transfers between devices with their start and end apart: 16, of which 2 were waited for; matrix products, arithmetic and copies ran while one was open for 8% of the time, Pallas kernels for 0%

commit v1 on v0

v1 whole, which is shorter than its diff:
```python
import jax
import jax.numpy as jnp
from jax import lax
from jax.experimental import pallas as pl
from jax.experimental.pallas import tpu as pltpu
from jax.sharding import PartitionSpec as P

ITERS = 6
HALO = 8
LANES = 128
F32 = jnp.float32
BF16 = jnp.bfloat16


def iota(shape, dim):
    return lax.broadcasted_iota(jnp.int32, shape, dim)


def split3(x):
    a = x.astype(BF16).astype(F32)
    r = x - a
    b = r.astype(BF16).astype(F32)
    return a, b, r - b


def land_kernel(precip, pet, soil_init, ksat, land_mask, soil_out, msg, turned):
    mask = land_mask[...].astype(F32)
    p = precip[...]
    s0 = soil_init[...]
    k = ksat[...]
    wet = 2.0 * s0
    cap = k * (1.0 - wet)
    runoff = mask * p * p / (p + cap)
    wet2 = wet * wet
    drainage = 0.25 * mask * k * (wet2 * wet2)
    evap = mask * pet[...] * wet
    soil_out[...] = s0 + 0.1 * (mask * p - runoff - drainage - evap)
    rows = p.shape[1]
    fields = jnp.concatenate([runoff, drainage], axis=0)
    turned[0:8, :] = jnp.zeros((8, LANES), F32)
    turned[rows + 8 : rows + 16, :] = jnp.zeros((8, LANES), F32)
    turned[8 : rows + 8, :] = jnp.concatenate([fields] * 4, axis=0).T
    group = iota((32, LANES), 1) // 32
    for j in range(3):
        chunk = None
        for q in range(4):
            part = turned[pl.ds(6 + 4 * j + q, 32, stride=8), :]
            chunk = part if q == 0 else jnp.where(group == q, part, chunk)
        msg[:, LANES * j : LANES * (j + 1)] = chunk


def route_kernel(
    land, head_init, sub_init, conduct, drain, code, share, slot, places, above, below,
    head_out, sub_out, msg,
    turned, h_a, h_b, s_a, s_b, g_w, a_w, dn_w, up_w, rt_w, lf_w, kp_w, parts,
):
    width = head_init.shape[1]
    tiles = width // LANES
    rows = 32 + 2 * HALO
    lane = iota((rows, LANES), 1)
    first = lane == 0
    last = lane == LANES - 1
    zero = jnp.zeros((rows, LANES), F32)

    a, b, c = split3(land[...])
    stacked = jnp.concatenate([a, b, c, jnp.zeros_like(a)], axis=0)
    turned[...] = stacked.T
    lhs = jnp.concatenate([turned[pl.ds(q, 24, stride=16), :] for q in range(16)], axis=0)
    lhs = lhs.astype(BF16)
    low_half = iota((8, 256), 0) < 4
    src = iota((LANES, 256), 0)
    dst = iota((LANES, 256), 1)
    col = (iota((24, 256), 1) & 63) >> 2
    for n in range(width // 256):
        hot = ((src & 31) == ((dst + 256 * n) >> 6)) & (src < 96)
        spread = jnp.dot(lhs, jnp.where(hot, 1.0, 0.0).astype(BF16), preferred_element_type=F32)
        fine = spread[0:24]
        for q in range(1, 16):
            fine = jnp.where(col == q, spread[24 * q : 24 * q + 24], fine)
        at = slice(256 * n, 256 * n + 256)
        for i in range(6):
            if i == 0:
                h0, s0 = above[0:8, at], above[8:16, at]
            elif i == 5:
                h0, s0 = below[0:8, at], below[8:16, at]
            else:
                h0, s0 = head_init[8 * i - 8 : 8 * i, at], sub_init[8 * i - 8 : 8 * i, at]
            here = slice(8 * i, 8 * i + 8)
            h_a[here, at] = h0 + jnp.where(low_half, fine[4 * i : 4 * i + 1], fine[4 * i + 2 : 4 * i + 3])
            s_a[here, at] = s0 + jnp.where(low_half, fine[4 * i + 1 : 4 * i + 2], fine[4 * i + 3 : 4 * i + 4])

    def window(own, field, at):
        lo = 8 * field
        return jnp.concatenate([above[lo : lo + 8, at], own[:, at], below[lo : lo + 8, at]], axis=0)

    def cut(j):
        return slice(LANES * j, LANES * (j + 1))

    for j in range(tiles):
        at = cut(j)
        d = window(drain, 3, at)
        k = jnp.concatenate(
            [above[32:40, at], code[:, at].astype(F32), below[32:40, at]], axis=0
        )
        moves = []
        for value, ref in ((0.0, dn_w), (1.0, up_w), (2.0, rt_w), (3.0, lf_w)):
            part = jnp.where(k == value, d, 0.0)
            ref[:, at] = part
            moves.append(part)
        kp_w[:, at] = 1.0 - (moves[0] + moves[1] + moves[2] + moves[3])
        g_w[:, at] = window(conduct, 2, at)
    for j in range(tiles):
        at = cut(j)
        g = g_w[:, at]
        left = pltpu.roll(g_w[:, cut(j - 1)], 1, 1) if j > 0 else zero
        right = pltpu.roll(g_w[:, cut(j + 1)], LANES - 1, 1) if j < tiles - 1 else zero
        total = pltpu.roll(g, 1, 0) + pltpu.roll(g, rows - 1, 0)
        total = total + jnp.where(first, left, pltpu.roll(g, 1, 1))
        total = total + jnp.where(last, right, pltpu.roll(g, LANES - 1, 1))
        a_w[:, at] = 1.0 - g * total

    def products(j, h_in, s_in):
        at = cut(j)
        p = g_w[:, at] * h_in[:, at]
        s = s_in[:, at]
        return (
            p,
            pltpu.roll(p, 1, 1),
            pltpu.roll(p, LANES - 1, 1),
            pltpu.roll(rt_w[:, at] * s, 1, 1),
            pltpu.roll(lf_w[:, at] * s, LANES - 1, 1),
        )

    def substep(h_in, s_in, h_to, s_to):
        before = (zero,) * 5
        now = products(0, h_in, s_in)
        for j in range(tiles):
            at = cut(j)
            after = products(j + 1, h_in, s_in) if j < tiles - 1 else (zero,) * 5
            p = now[0]
            s = s_in[:, at]
            flux = pltpu.roll(p, 1, 0) + pltpu.roll(p, rows - 1, 0)
            flux = flux + jnp.where(first, before[1], now[1])
            flux = flux + jnp.where(last, after[2], now[2])
            h_to[:, at] = a_w[:, at] * h_in[:, at] + g_w[:, at] * flux
            new = kp_w[:, at] * s
            new = new + pltpu.roll(dn_w[:, at] * s, 1, 0)
            new = new + pltpu.roll(up_w[:, at] * s, rows - 1, 0)
            new = new + jnp.where(first, before[3], now[3])
            new = new + jnp.where(last, after[4], now[4])
            s_to[:, at] = new
            before, now = now, after

    def pair(i, carry):
        substep(h_a, s_a, h_b, s_b)
        substep(h_b, s_b, h_a, s_a)
        return carry

    lax.fori_loop(0, ITERS // 2, pair, 0)

    own = slice(HALO, HALO + 32)
    sub_out[...] = s_a[own, :]
    for j in range(tiles):
        at = cut(j)
        h = h_a[own, at]
        inflow = share[:, at] * h
        head_out[:, at] = h - inflow
        v1, v2, v3 = split3(inflow)
        parts[0, :, at] = v1
        parts[1, :, at] = v2
        parts[2, :, at] = v3
        k = slot[:, at]
        parts[3, :, at] = (k >> 6).astype(F32)
        parts[4, :, at] = (k & 63).astype(F32)

    owner = iota((32, width), 0).astype(F32).astype(BF16)
    place = iota((64, width), 0).astype(F32).astype(BF16)
    one = jnp.ones((64, width), BF16)
    none64 = jnp.zeros((64, width), BF16)
    none32 = jnp.zeros((32, width), BF16)

    def row(r, total):
        def wide(i, n):
            return jnp.broadcast_to(parts[i, pl.ds(r, 1), :], (n, width)).astype(BF16)

        hi = wide(3, 32) == owner
        lhs = jnp.concatenate([jnp.where(hi, wide(i, 32), none32) for i in range(3)], axis=0)
        rhs = jnp.where(wide(4, 64) == place, one, none64)
        return total + lax.dot_general(lhs, rhs, (((1,), (1,)), ((), ())), preferred_element_type=F32)

    total = lax.fori_loop(0, 32, row, jnp.zeros((96, 64), F32))
    total = total[0:32] + total[32:64] + total[64:96]
    p = places[...].astype(F32)
    turned[pl.ds(0, 16, stride=2), :] = pltpu.roll(p, 64, 1)
    turned[pl.ds(1, 16, stride=2), :] = p
    wide = jnp.concatenate([total, jnp.zeros_like(total)], axis=1)
    msg[...] = jnp.where(iota((32, LANES), 1) < 64, wide, turned[0:32, :])


def reach_kernel(got, out, stage):
    data = got[...]
    valid = iota(data.shape, 1) < 64
    place = pltpu.roll(data, 64, 1).astype(jnp.int32)
    a, b, c = split3(jnp.where(valid, data, 0.0))
    stage[0] = a
    stage[1] = b
    stage[2] = c
    stage[3] = (place >> 7).astype(F32)
    stage[4] = (place & 127).astype(F32)
    hi_line = iota((16, LANES), 0).astype(F32)
    lo_line = iota((128, LANES), 0).astype(F32)
    total = jnp.zeros((48, LANES), F32)
    for u in range(data.shape[0]):
        hi = stage[3, u : u + 1, :] == hi_line
        lhs = jnp.concatenate(
            [jnp.where(hi, stage[i, u : u + 1, :], 0.0) for i in range(3)], axis=0
        ).astype(BF16)
        rhs = jnp.where(stage[4, u : u + 1, :] == lo_line, 1.0, 0.0).astype(BF16)
        total = total + lax.dot_general(
            lhs, rhs, (((1,), (1,)), ((), ())), preferred_element_type=F32
        )
    out[...] = total[0:16] + total[16:32] + total[32:48]


def local(
    precip,
    pet,
    soil_init,
    ksat,
    land_mask,
    head_init,
    subsurface_init,
    conduct,
    drain_rate,
    flow_code,
    channel_share,
    cell_slot,
    slot_reach,
):
    vmem = pl.BlockSpec(memory_space=pltpu.VMEM)
    peers = lax.axis_size("tile")
    width = head_init.shape[1]
    grid = (head_init, subsurface_init, conduct, drain_rate, flow_code)
    up = [(i, i + 1) for i in range(peers - 1)]
    down = [(j, i) for i, j in up]
    bottom = jnp.concatenate([x[-HALO:].astype(F32) for x in grid], axis=0)
    top = jnp.concatenate([x[:HALO].astype(F32) for x in grid], axis=0)
    above = lax.ppermute(bottom, "tile", up)
    below = lax.ppermute(top, "tile", down)

    soil, land = pl.pallas_call(
        land_kernel,
        out_shape=(
            jax.ShapeDtypeStruct(precip.shape, F32),
            jax.ShapeDtypeStruct((peers, 384), F32),
        ),
        in_specs=[vmem] * 5,
        out_specs=(vmem, vmem),
        scratch_shapes=[pltpu.VMEM((precip.shape[1] + 16, LANES), F32)],
        name="land_step",
    )(precip, pet, soil_init, ksat, land_mask)
    land = lax.all_to_all(land, "tile", split_axis=0, concat_axis=0, tiled=True)

    window = pltpu.VMEM((32 + 2 * HALO, width), F32)
    head, sub, sums = pl.pallas_call(
        route_kernel,
        out_shape=(
            jax.ShapeDtypeStruct(head_init.shape, F32),
            jax.ShapeDtypeStruct(head_init.shape, F32),
            jax.ShapeDtypeStruct((peers, LANES), F32),
        ),
        in_specs=[vmem] * 11,
        out_specs=(vmem, vmem, vmem),
        scratch_shapes=[pltpu.VMEM((384, LANES), F32)]
        + [window] * 11
        + [pltpu.VMEM((5, 32, width), F32)],
        compiler_params=pltpu.CompilerParams(vmem_limit_bytes=48 * 1024 * 1024),
        name="route",
    )(
        land, head_init, subsurface_init, conduct, drain_rate, flow_code, channel_share,
        cell_slot, slot_reach.reshape(-1, LANES), above, below,
    )
    sums = lax.all_to_all(sums, "tile", split_axis=0, concat_axis=0, tiled=True)
    reach = pl.pallas_call(
        reach_kernel,
        out_shape=jax.ShapeDtypeStruct((16, LANES), F32),
        in_specs=[vmem],
        out_specs=vmem,
        scratch_shapes=[pltpu.VMEM((5, peers, LANES), F32)],
        name="reach_sums",
    )(sums)
    return (soil, head, sub, reach.reshape(-1))


def solution(mesh):
    rows = P(("member", "tile"), None)
    flat = P(("member", "tile"))
    return jax.shard_map(
        local,
        mesh=mesh,
        in_specs=(rows,) * 12 + (flat,),
        out_specs=(rows, rows, rows, flat),
        check_vma=False,
    )
```

time: 570 us -> 60.8 us (0.11); the launches traced: 564 us -> 60.3 us
  waiting for transfers between devices: 225 us -> 0.01 us
  other arithmetic: 158 us -> 0.01 us
  local copies, waits for them, and re-layouts: 109 us -> 4.48 us
  starting transfers between devices: 53.7 us -> 6.65 us
  blocking collectives: 0 us -> 30.7 us
  Pallas kernels: 0 us -> 17.7 us
  between operations: 16 us -> 0.74 us
    unnamed x2 -> x0, waiting for transfers between devices: 221 us -> none
    reduce_sum x33 -> x0, other arithmetic: 81.1 us -> none  [the longest x32 78.1 us: add_block(): jnp.sum(jnp.where(hit, block_values[:, None], 0.0), axis=0)]
    add x44 -> x0, other arithmetic: 37 us -> none  [the longest x5 27.3 us: advance(): h_new = hc + gc * flux]
    ppermute x14 -> x2, starting transfers between devices: 42.4 us -> 6.65 us  [the longest x1 4.73 us: local(): above = lax.ppermute(bottom, 'tile', up)]
    all_to_all x0 -> x2, blocking collectives: none -> 30.7 us  [the longest x1 19.2 us: local(): land = lax.all_to_all(land, 'tile', split_axis=0, concat_axis=0, tiled=True)]
    dynamic_slice x64 -> x0, local copies, waits for them, and re-layouts: 27.8 us -> none  [slot_totals(): lax.scan(add_block, jnp.zeros((slots,), jnp.float32), (inflow, cell_slot))]
    unnamed x167 -> x21, local copies, waits for them, and re-layouts: 30.6 us -> 3.63 us
    slice x14 -> x0, local copies, waits for them, and re-layouts: 25 us -> none  [the longest x6 13.3 us: padded(): first = lax.slice_in_dim(x, 0, width, axis=dim)]
  transfers between devices with their start and end apart: 16 -> 2, of which waited for: 2 -> 0; matrix products, arithmetic and copies ran while one was open for 8% -> 1% of each run, Pallas kernels for 0% -> 3%
where the time goes in v1:
time: 60.8 us; the launch traced here: 60.3 us
  blocking collectives  30.7 us (50%)
  Pallas kernels  17.7 us (29%)
  starting transfers between devices  6.65 us (11%)
  local copies, waits for them, and re-layouts  4.48 us (7%)
  between operations  0.74 us (1%)
    all_to_all x1, blocking collectives, local(): land = lax.all_to_all(land, 'tile', split_axis=0, concat_axis=0, tiled=True)  19.2 us
    pallas_call x1, Pallas kernels, local(): pl.pallas_call(route_kernel, out_shape=(jax.ShapeDtypeStruct(head_init.sh...  14 us
    all_to_all x1, blocking collectives, local(): sums = lax.all_to_all(sums, 'tile', split_axis=0, concat_axis=0, tiled=True)  11.5 us
    ppermute x1, starting transfers between devices, local(): above = lax.ppermute(bottom, 'tile', up)  4.73 us
    unnamed x21, local copies, waits for them, and re-layouts  3.63 us
    pallas_call x1, Pallas kernels, local(): pl.pallas_call(reach_kernel, out_shape=jax.ShapeDtypeStruct((16, LANES),...  2.16 us
    ppermute x1, starting transfers between devices, local(): below = lax.ppermute(top, 'tile', down)  1.92 us
    pallas_call x1, Pallas kernels, local(): pl.pallas_call(land_kernel, out_shape=(jax.ShapeDtypeStruct(precip.shape,...  1.54 us
  transfers between devices with their start and end apart: 2, of which 0 were waited for; matrix products, arithmetic and copies ran while one was open for 1% of the time, Pallas kernels for 3%

profile of v1, /device:TPU:1, one launch (start us, length us, event | category | flops | bytes accessed | tf_op | source)
XLA Modules:
  0.0 60.3 jit_solution(8124308851141390335)
XLA Ops:
  0.6 0.0 copy-start.1
  0.6 0.0 copy-start.2
  0.7 0.9 %slice_dynamic-update-slice_fusion.3 = (f32[40,2048]{1,0:T(8,128)S(1)}, f32[40,2048]{1,0:T(8,128)S(1)}) fusion(f32[32,2048]{1,0:T(8,128)} %head_init.1), kind=kLoop, calls=%fused_computation.4 | loop fusion | bytes 262144
  1.6 0.0 copy-done.1
  1.6 0.0 copy-start.3
  1.6 0.1 copy-done.2
  1.7 0.0 copy-start.4
  1.7 0.8 %copy-done.3 = f32[32,2048]{1,0:T(8,128)S(1)} copy-done((f32[32,2048]{1,0:T(8,128)S(1)}, f32[32,2048]{1,0:T(8,128)}, u32[]{:S(2)}) %copy-start.3) | copy-done | bytes 262168
  2.6 0.1 copy-done.4
  2.7 0.0 copy-start
  2.7 0.0 copy-start.5
  2.7 4.7 %collective-permute-start = (f32[40,2048]{1,0:T(8,128)S(1)}, f32[40,2048]{1,0:T(8,128)S(1)}, u32[]{:S(2)}, u32[]{:S(2)}) collective-permute-start(f32[40,2048]{1,0:T(8,128)S(1)} %get-tuple-element.15), channel_id=1, source_target_pairs={{0,1},{1,2},{2,3},{3,4},{4,5},{5,6},{6,7},{7,8},{8,9},{9,10},{10,1... | collective-permute-start | bytes 983048 | tf_op jit(solution)/shard_map/ppermute | solution.py:248
  7.4 1.9 %collective-permute-start.1 = (f32[40,2048]{1,0:T(8,128)S(1)}, f32[40,2048]{1,0:T(8,128)S(1)}, u32[]{:S(2)}, u32[]{:S(2)}) collective-permute-start(f32[40,2048]{1,0:T(8,128)S(1)} %get-tuple-element.14), channel_id=1, source_target_pairs={{1,0},{2,1},{3,2},{4,3},{5,4},{6,5},{7,6},{8,7},{9,8},{10,9},{11,1... | collective-permute-start | bytes 983048 | tf_op jit(solution)/shard_map/ppermute | solution.py:249
  9.4 1.5 %land_step.1 = (f32[16,256]{1,0:T(8,128)}, f32[32,384]{1,0:T(8,128)}) custom-call(f32[16,256]{1,0:T(8,128)} %precip.1, f32[16,256]{1,0:T(8,128)} %pet.1, f32[16,256]{1,0:T(8,128)} %soil_init.1, f32[16,256]{1,0:T(8,128)} %ksat.1, s32[16,256]{1,0:T(8,128)} %land_mask.1), custom_call_target="tpu_custom_call" | custom-call | tf_op jit(solution)/shard_map/land_step/pallas_call | solution.py:251
  10.9 0.8 %copy.17 = f32[32,1,384]{2,1,0:T(1,128)S(1)} copy(f32[32,1,384]{2,0,1:T(8,128)} %bitcast.14) | data formatting | bytes 98304 | tf_op jit(solution)/shard_map/all_to_all | solution.py:262
  11.8 19.2 %all_to_all.22 = f32[32,1,384]{2,1,0:T(1,128)S(1)} all-to-all(f32[32,1,384]{2,1,0:T(1,128)S(1)} %copy.17), channel_id=1, replica_groups=mesh['member'=8,'tile'=32] {'tile'}, dimensions={0} | all-to-all | bytes 98304 | tf_op jit(solution)/shard_map/all_to_all | solution.py:262
  31.0 0.0 copy-start.7
  31.0 0.0 collective-permute-done.above
  31.0 0.0 collective-permute-done.1.below
  31.0 0.0 copy-done
  31.0 0.0 copy-done.5
  31.0 0.7 %copy-done.7 = s32[2048]{0:T(1024)S(1)} copy-done((s32[2048]{0:T(1024)S(1)}, s32[2048]{0:T(1024)}, u32[]{:S(2)}) %copy-start.7) | copy-done | bytes 8216
  31.7 0.0 copy-start.6
  31.7 0.9 %copy-done.6 = s32[32,2048]{1,0:T(8,128)S(1)} copy-done((s32[32,2048]{1,0:T(8,128)S(1)}, s32[32,2048]{1,0:T(8,128)}, u32[]{:S(2)}) %copy-start.6) | copy-done | bytes 262168
  32.7 14.0 %route.1 = (f32[32,2048]{1,0:T(8,128)}, f32[32,2048]{1,0:T(8,128)}, f32[32,128]{1,0:T(8,128)S(1)}) custom-call(f32[32,384]{1,0:T(8,128)S(1)} %bitcast.10, f32[32,2048]{1,0:T(8,128)S(1)} %copy-done, f32[32,2048]{1,0:T(8,128)S(1)} %copy-done.1, f32[32,2048]{1,0:T(8,128)S(1)} %copy-done.2, f32[32,2048]{1,0:T(8,128)S(1)} %copy-done.3, s32[32,2048]{1,0:T(8,128)S(1)} %copy-done.4, ...), custom_call_target="tpu_custom_call" | custom-call | tf_op jit(solution)/shard_map/route/pallas_call | solution.py:265
  46.7 11.5 %all_to_all.23 = f32[32,1,128]{2,1,0:T(1,128)} all-to-all(f32[32,1,128]{2,1,0:T(1,128)S(1)} %bitcast.11), channel_id=1, replica_groups=mesh['member'=8,'tile'=32] {'tile'}, dimensions={0} | all-to-all | bytes 32768 | tf_op jit(solution)/shard_map/all_to_all | solution.py:283
  58.1 2.2 %reach_sums.1 = f32[16,128]{1,0:T(8,128)} custom-call(f32[32,128]{1,0:T(8,128)} %bitcast.13), custom_call_target="tpu_custom_call" | custom-call | tf_op jit(solution)/shard_map/reach_sums/pallas_call | solution.py:284
  (5 shorter events, 0.0 us)
Async XLA Ops:
  0.6 1.0 %copy-start.1 = (f32[32,2048]{1,0:T(8,128)S(1)}, f32[32,2048]{1,0:T(8,128)}, u32[]{:S(2)}) copy-start(f32[32,2048]{1,0:T(8,128)} %sub_init.1) | copy-start | bytes 786436
  0.6 1.1 %copy-start.2 = (f32[32,2048]{1,0:T(8,128)S(1)}, f32[32,2048]{1,0:T(8,128)}, u32[]{:S(2)}) copy-start(f32[32,2048]{1,0:T(8,128)} %conduct.1) | copy-start | bytes 786436
  1.6 1.0 %copy-start.3 = (f32[32,2048]{1,0:T(8,128)S(1)}, f32[32,2048]{1,0:T(8,128)}, u32[]{:S(2)}) copy-start(f32[32,2048]{1,0:T(8,128)} %drain.1) | copy-start | bytes 786436
  1.7 1.0 %copy-start.4 = (s32[32,2048]{1,0:T(8,128)S(1)}, s32[32,2048]{1,0:T(8,128)}, u32[]{:S(2)}) copy-start(s32[32,2048]{1,0:T(8,128)} %code.1) | copy-start | bytes 786436
  2.7 28.3 %copy-start = (f32[32,2048]{1,0:T(8,128)S(1)}, f32[32,2048]{1,0:T(8,128)}, u32[]{:S(2)}) copy-start(f32[32,2048]{1,0:T(8,128)} %head_init.1) | copy-start | bytes 786436
  2.7 28.3 %copy-start.5 = (f32[32,2048]{1,0:T(8,128)S(1)}, f32[32,2048]{1,0:T(8,128)}, u32[]{:S(2)}) copy-start(f32[32,2048]{1,0:T(8,128)} %share.1) | copy-start | bytes 786436
  2.7 28.3 %collective-permute-start = (f32[40,2048]{1,0:T(8,128)S(1)}, f32[40,2048]{1,0:T(8,128)S(1)}, u32[]{:S(2)}, u32[]{:S(2)}) collective-permute-start(f32[40,2048]{1,0:T(8,128)S(1)} %get-tuple-element.15), channel_id=1, source_target_pairs={{0,1},{1,2},{2,3},{3,4},{4,5},{5,6},{6,7},{7,8},{8,9},{9,10},{10,1... | collective-permute-start | bytes 983048 | tf_op jit(solution)/shard_map/ppermute | solution.py:248
  7.4 23.6 %collective-permute-start.1 = (f32[40,2048]{1,0:T(8,128)S(1)}, f32[40,2048]{1,0:T(8,128)S(1)}, u32[]{:S(2)}, u32[]{:S(2)}) collective-permute-start(f32[40,2048]{1,0:T(8,128)S(1)} %get-tuple-element.14), channel_id=1, source_target_pairs={{1,0},{2,1},{3,2},{4,3},{5,4},{6,5},{7,6},{8,7},{9,8},{10,9},{11,1... | collective-permute-start | bytes 983048 | tf_op jit(solution)/shard_map/ppermute | solution.py:249
  31.0 0.7 %copy-start.7 = (s32[2048]{0:T(1024)S(1)}, s32[2048]{0:T(1024)}, u32[]{:S(2)}) copy-start(s32[2048]{0:T(1024)} %param.25) | copy-start | bytes 24580
  31.7 0.9 %copy-start.6 = (s32[32,2048]{1,0:T(8,128)S(1)}, s32[32,2048]{1,0:T(8,128)}, u32[]{:S(2)}) copy-start(s32[32,2048]{1,0:T(8,128)} %slot.1) | copy-start | bytes 786436

commit v2 on v1

v2 whole, which is shorter than its diff:
```python
import jax
import jax.numpy as jnp
from jax import lax
from jax.experimental import pallas as pl
from jax.experimental.pallas import tpu as pltpu
from jax.sharding import PartitionSpec as P

ITERS = 6
HALO = 8
OWN = 32
ROWS = OWN + 2 * HALO
LANES = 128
F32 = jnp.float32
BF16 = jnp.bfloat16
MIB = 1024 * 1024


def iota(shape, dim):
    return lax.broadcasted_iota(jnp.int32, shape, dim)


def split3(x):
    a = x.astype(BF16).astype(F32)
    r = x - a
    b = r.astype(BF16).astype(F32)
    return a, b, r - b


def cut(j):
    return slice(LANES * j, LANES * (j + 1))


def left_of(tile, before):
    return jnp.where(iota(tile.shape, 1) == 0, before, tile)


def right_of(tile, after):
    return jnp.where(iota(tile.shape, 1) == LANES - 1, after, tile)


def send_kernel(
    precip, pet, soil_init, ksat, land_mask, places, head, sub, conduct, drain, code,
    soil_out, msg, top, bottom, turned, fields_in, mask_in, place_in, code_edge, sem,
):
    local = []
    for i, ref in enumerate((precip, pet, soil_init, ksat)):
        local.append(pltpu.make_async_copy(ref, fields_in.at[i], sem.at[10 + i]))
    local.append(pltpu.make_async_copy(land_mask, mask_in, sem.at[14]))
    local.append(pltpu.make_async_copy(places, place_in, sem.at[15]))
    copies = []
    for i, ref in enumerate((head, sub, conduct, drain)):
        into = slice(8 * i, 8 * i + 8)
        copies.append(pltpu.make_async_copy(ref.at[24:32, :], bottom.at[into, :], sem.at[2 * i]))
        copies.append(pltpu.make_async_copy(ref.at[0:8, :], top.at[into, :], sem.at[2 * i + 1]))
    codes = (
        pltpu.make_async_copy(code.at[24:32, :], code_edge.at[0], sem.at[8]),
        pltpu.make_async_copy(code.at[0:8, :], code_edge.at[1], sem.at[9]),
    )
    for c in local:
        c.start()
    for c in codes:
        c.start()
    for c in copies:
        c.start()
    for c in local:
        c.wait()
    mask = mask_in[...].astype(F32)
    p = fields_in[0]
    s0 = fields_in[2]
    k = fields_in[3]
    wet = 2.0 * s0
    cap = k * (1.0 - wet)
    runoff = mask * p * p / (p + cap)
    wet2 = wet * wet
    drainage = 0.25 * mask * k * (wet2 * wet2)
    evap = mask * fields_in[1] * wet
    soil_out[...] = s0 + 0.1 * (mask * p - runoff - drainage - evap)
    rows = p.shape[1]
    fields = jnp.concatenate([runoff, drainage], axis=0)
    turned[0:8, :] = jnp.zeros((8, LANES), F32)
    turned[rows + 8 : rows + 16, :] = jnp.zeros((8, LANES), F32)
    turned[8 : rows + 8, :] = jnp.concatenate([fields] * 4, axis=0).T
    group = iota((32, LANES), 1) // 32
    for j in range(3):
        chunk = None
        for q in range(4):
            part = turned[pl.ds(6 + 4 * j + q, 32, stride=8), :]
            chunk = part if q == 0 else jnp.where(group == q, part, chunk)
        msg[pl.ds(j, 32, stride=4), :] = chunk
    place = place_in[...].astype(F32)
    msg[pl.ds(3, 16, stride=8), :] = place
    msg[pl.ds(7, 16, stride=8), :] = pltpu.roll(place, 64, 1)
    for c in codes:
        c.wait()
    bottom[32:40, :] = code_edge[0].astype(F32)
    top[32:40, :] = code_edge[1].astype(F32)
    for c in copies:
        c.wait()


def route_kernel(
    land, head_init, sub_init, conduct, drain, code, above, below, share, slot,
    head_out, sub_out, msg,
    turned, h_a, h_b, s_a, s_b, g_w, a_w, dn_w, up_w, rt_w, lf_w, kp_w,
    head, sub, shares, slots, parts, sem,
):
    tiles = g_w.shape[0]
    width = tiles * LANES
    zero = jnp.zeros((ROWS, LANES), F32)
    share_copy = pltpu.make_async_copy(share, shares, sem.at[0])
    slot_copy = pltpu.make_async_copy(slot, slots, sem.at[3])
    share_copy.start()
    slot_copy.start()

    def window(own, field, j):
        lo = 8 * field
        at = cut(j)
        return jnp.concatenate(
            [above[lo : lo + 8, at], own[:, at].astype(F32), below[lo : lo + 8, at]], axis=0
        )

    for j in range(tiles):
        g_w[j] = window(conduct, 2, j)
        d = window(drain, 3, j)
        k = window(code, 4, j)
        moves = [jnp.where(k == float(i), d, 0.0) for i in range(4)]
        dn_w[j], up_w[j], rt_w[j], lf_w[j] = moves
        kp_w[j] = 1.0 - (moves[0] + moves[1] + moves[2] + moves[3])
    for j in range(tiles):
        g = g_w[j]
        left = pltpu.roll(g_w[j - 1], 1, 1) if j > 0 else zero
        right = pltpu.roll(g_w[j + 1], LANES - 1, 1) if j < tiles - 1 else zero
        total = pltpu.roll(g, 1, 0) + pltpu.roll(g, ROWS - 1, 0)
        total = total + left_of(pltpu.roll(g, 1, 1), left)
        total = total + right_of(pltpu.roll(g, LANES - 1, 1), right)
        a_w[j] = 1.0 - g * total

    data = jnp.concatenate([land[pl.ds(j, 32, stride=4), :] for j in range(3)], axis=1)
    a, b, c = split3(data)
    turned[...] = jnp.concatenate([a, b, c, jnp.zeros_like(a)], axis=0).T
    lhs = jnp.concatenate([turned[pl.ds(q, 24, stride=16), :] for q in range(16)], axis=0)
    lhs = lhs.astype(BF16)
    low_half = iota((8, 256), 0) < 4
    src = iota((LANES, 256), 0)
    dst = iota((LANES, 256), 1)
    col = (iota((24, 256), 1) & 63) >> 2
    for n in range(width // 256):
        hot = ((src & 31) == ((dst + 256 * n) >> 6)) & (src < 96)
        spread = jnp.dot(lhs, jnp.where(hot, 1.0, 0.0).astype(BF16), preferred_element_type=F32)
        fine = spread[0:24]
        for q in range(1, 16):
            fine = jnp.where(col == q, spread[24 * q : 24 * q + 24], fine)
        for i in range(ROWS // 8):
            here = slice(8 * i, 8 * i + 8)
            at = slice(256 * n, 256 * n + 256)
            if i == 0:
                h0, s0 = above[0:8, at], above[8:16, at]
            elif i == ROWS // 8 - 1:
                h0, s0 = below[0:8, at], below[8:16, at]
            else:
                rows = slice(8 * i - 8, 8 * i)
                h0, s0 = head_init[rows, at], sub_init[rows, at]
            r = 4 * i
            h0 = h0 + jnp.where(low_half, fine[r : r + 1], fine[r + 2 : r + 3])
            s0 = s0 + jnp.where(low_half, fine[r + 1 : r + 2], fine[r + 3 : r + 4])
            for u in range(2):
                j = 2 * n + u
                h_a[j, here, :] = h0[:, cut(u)]
                s_a[j, here, :] = s0[:, cut(u)]

    def products(j, h_in, s_in):
        p = g_w[j] * h_in[j]
        s = s_in[j]
        return (
            p,
            pltpu.roll(p, 1, 1),
            pltpu.roll(p, LANES - 1, 1),
            pltpu.roll(rt_w[j] * s, 1, 1),
            pltpu.roll(lf_w[j] * s, LANES - 1, 1),
        )

    def substep(h_in, s_in, h_to, s_to):
        before = (zero,) * 5
        now = products(0, h_in, s_in)
        for j in range(tiles):
            after = products(j + 1, h_in, s_in) if j < tiles - 1 else (zero,) * 5
            p = now[0]
            s = s_in[j]
            flux = pltpu.roll(p, 1, 0) + pltpu.roll(p, ROWS - 1, 0)
            flux = flux + left_of(now[1], before[1])
            flux = flux + right_of(now[2], after[2])
            h_to[j] = a_w[j] * h_in[j] + g_w[j] * flux
            new = pltpu.roll(dn_w[j] * s, 1, 0) + pltpu.roll(up_w[j] * s, ROWS - 1, 0)
            new = new + kp_w[j] * s
            new = new + left_of(now[3], before[3])
            s_to[j] = new + right_of(now[4], after[4])
            before, now = now, after

    for i in range(ITERS // 2):
        substep(h_a, s_a, h_b, s_b)
        substep(h_b, s_b, h_a, s_a)

    share_copy.wait()
    slot_copy.wait()
    for j in range(tiles):
        at = cut(j)
        h = h_a[j, HALO : HALO + OWN, :]
        sub[:, at] = s_a[j, HALO : HALO + OWN, :]
        inflow = shares[:, at] * h
        head[:, at] = h - inflow
        parts[0, :, at], parts[1, :, at], parts[2, :, at] = split3(inflow)
        q = slots[:, at]
        parts[3, :, at] = (q >> 6).astype(F32)
        parts[4, :, at] = (q & 63).astype(F32)
    head_copy = pltpu.make_async_copy(head, head_out, sem.at[1])
    sub_copy = pltpu.make_async_copy(sub, sub_out, sem.at[2])
    head_copy.start()
    sub_copy.start()

    owner = iota((32, width), 0).astype(F32).astype(BF16)
    place = iota((64, width), 0).astype(F32).astype(BF16)
    one = jnp.ones((64, width), BF16)
    none64 = jnp.zeros((64, width), BF16)
    none32 = jnp.zeros((32, width), BF16)

    def wide(row, n):
        return jnp.broadcast_to(row, (n, width)).astype(BF16)

    total = jnp.zeros((96, 64), F32)
    for r in range(OWN):
        at = slice(r, r + 1)
        hi = wide(parts[3, at, :], 32) == owner
        lhs = jnp.concatenate(
            [jnp.where(hi, wide(parts[i, at, :], 32), none32) for i in range(3)], axis=0
        )
        rhs = jnp.where(wide(parts[4, at, :], 64) == place, one, none64)
        total = total + lax.dot_general(
            lhs, rhs, (((1,), (1,)), ((), ())), preferred_element_type=F32
        )
    total = total[0:32] + total[32:64] + total[64:96]
    msg[...] = jnp.concatenate([total, jnp.zeros_like(total)], axis=1)
    head_copy.wait()
    sub_copy.wait()


def reach_kernel(land, got, out):
    low = iota((16, LANES), 1) < 64

    def pack(x):
        return jnp.where(low, x[0:16], pltpu.roll(x[16:32], 64, 1))

    sums = pack(got[...])
    place = pack(land[pl.ds(3, 32, stride=4), :]).astype(jnp.int32)

    def line(x):
        return jnp.concatenate([x[u : u + 1] for u in range(16)], axis=1)

    width = 16 * LANES
    hi = line((place >> 7).astype(F32)) == iota((16, width), 0).astype(F32)
    lhs = jnp.concatenate([jnp.where(hi, line(x), 0.0) for x in split3(sums)], axis=0)
    lo = line((place & 127).astype(F32)) == iota((LANES, width), 0).astype(F32)
    total = lax.dot_general(
        lhs.astype(BF16), jnp.where(lo, 1.0, 0.0).astype(BF16),
        (((1,), (1,)), ((), ())), preferred_element_type=F32,
    )
    out[...] = total[0:16] + total[16:32] + total[32:48]


def local(
    precip,
    pet,
    soil_init,
    ksat,
    land_mask,
    head_init,
    subsurface_init,
    conduct,
    drain_rate,
    flow_code,
    channel_share,
    cell_slot,
    slot_reach,
):
    vmem = pl.BlockSpec(memory_space=pltpu.VMEM)
    far = pl.BlockSpec(memory_space=pltpu.HBM)
    peers = lax.axis_size("tile")
    width = head_init.shape[1]
    tiles = width // LANES

    def hbm(x):
        return pltpu.with_memory_space_constraint(x, pltpu.HBM)

    def array(*shape):
        return jax.ShapeDtypeStruct(shape, F32)

    soil, msg, top, bottom = pl.pallas_call(
        send_kernel,
        out_shape=(
            array(*precip.shape), array(4 * peers, LANES), array(40, width), array(40, width),
        ),
        in_specs=[far] * 11,
        out_specs=(vmem,) * 4,
        scratch_shapes=[
            pltpu.VMEM((precip.shape[1] + 16, LANES), F32),
            pltpu.VMEM((4,) + precip.shape, F32),
            pltpu.VMEM(precip.shape, jnp.int32),
            pltpu.VMEM((16, LANES), jnp.int32),
            pltpu.VMEM((2, 8, width), jnp.int32),
            pltpu.SemaphoreType.DMA((16,)),
        ],
        compiler_params=pltpu.CompilerParams(vmem_limit_bytes=6 * MIB),
        name="send",
    )(
        *map(
            hbm,
            (
                precip, pet, soil_init, ksat, land_mask, slot_reach.reshape(-1, LANES),
                head_init, subsurface_init, conduct, drain_rate, flow_code,
            ),
        )
    )
    up = [(i, i + 1) for i in range(peers - 1)]
    down = [(j, i) for i, j in up]
    above = lax.ppermute(bottom, "tile", up)
    below = lax.ppermute(top, "tile", down)
    land = lax.all_to_all(
        msg.reshape(peers, 4, LANES), "tile", split_axis=0, concat_axis=0, tiled=True
    ).reshape(4 * peers, LANES)

    window = pltpu.VMEM((tiles, ROWS, LANES), F32)
    plane = pltpu.VMEM((OWN, width), F32)
    head, sub, sums = pl.pallas_call(
        route_kernel,
        out_shape=(array(OWN, width), array(OWN, width), array(peers, LANES)),
        in_specs=[vmem] * 8 + [far] * 2,
        out_specs=(far, far, vmem),
        scratch_shapes=[pltpu.VMEM((384, LANES), F32)]
        + [window] * 11
        + [plane] * 3
        + [pltpu.VMEM((OWN, width), jnp.int32), pltpu.VMEM((5, OWN, width), F32)]
        + [pltpu.SemaphoreType.DMA((4,))],
        compiler_params=pltpu.CompilerParams(vmem_limit_bytes=16 * MIB),
        name="route",
    )(
        land, head_init, subsurface_init, conduct, drain_rate, flow_code, above, below,
        hbm(channel_share), hbm(cell_slot),
    )
    sums = lax.all_to_all(sums, "tile", split_axis=0, concat_axis=0, tiled=True)
    reach = pl.pallas_call(
        reach_kernel,
        out_shape=array(16, LANES),
        in_specs=[vmem] * 2,
        out_specs=vmem,
        compiler_params=pltpu.CompilerParams(vmem_limit_bytes=6 * MIB),
        name="reach_sums",
    )(land, sums)
    return (soil, head, sub, reach.reshape(-1))


def solution(mesh):
    rows = P(("member", "tile"), None)
    flat = P(("member", "tile"))
    return jax.shard_map(
        local,
        mesh=mesh,
        in_specs=(rows,) * 12 + (flat,),
        out_specs=(rows, rows, rows, flat),
        check_vma=False,
    )
```

time: 60.8 us -> 49.4 us (0.81)
  Pallas kernels: 17.7 us -> 11.4 us
  local copies, waits for them, and re-layouts: 4.48 us -> 0.02 us
    pallas_call x3, Pallas kernels: 17.7 us -> 11.4 us  [the longest x1 8.46 us: local(): pl.pallas_call(route_kernel, out_shape=(array(OWN, width), array(OWN, wid...]
    unnamed x21 -> x10, local copies, waits for them, and re-layouts: 3.63 us -> 0.02 us
    all_to_all x1 -> x0, local copies, waits for them, and re-layouts: 0.85 us -> none  [local(): land = lax.all_to_all(land, 'tile', split_axis=0, concat_axis=0, tiled=True)]
  transfers between devices with their start and end apart: 2 -> 2, of which waited for: 0 -> 0; matrix products, arithmetic and copies ran while one was open for 1% -> 0% of each run, Pallas kernels for 3% -> 0%
where the time goes in v2:
time: 49.4 us; the launch traced here: 49.1 us
  blocking collectives  30.4 us (62%)
  Pallas kernels  11.4 us (23%)
  starting transfers between devices  6.52 us (13%)
  between operations  0.74 us (1%)
    all_to_all x1, blocking collectives, local(): lax.all_to_all(msg.reshape(peers, 4, LANES), 'tile', split_axis=0, concat...  19.4 us
    all_to_all x1, blocking collectives, local(): sums = lax.all_to_all(sums, 'tile', split_axis=0, concat_axis=0, tiled=True)  11 us
    pallas_call x1, Pallas kernels, local(): pl.pallas_call(route_kernel, out_shape=(array(OWN, width), array(OWN, wid...  8.46 us
    ppermute x1, starting transfers between devices, local(): above = lax.ppermute(bottom, 'tile', up)  4.59 us
    pallas_call x1, Pallas kernels, local(): pl.pallas_call(send_kernel, out_shape=(array(*precip.shape), array(4 * pe...  2 us
    ppermute x1, starting transfers between devices, local(): below = lax.ppermute(top, 'tile', down)  1.92 us
  transfers between devices with their start and end apart: 2, of which 0 were waited for; matrix products, arithmetic and copies ran while one was open for 0% of the time, Pallas kernels for 0%

profile of v2, /device:TPU:1, one launch (start us, length us, event | category | flops | bytes accessed | tf_op | source)
XLA Modules:
  0.0 49.1 jit_solution(13440808356107269704)
XLA Ops:
  0.6 0.0 copy-start
  0.6 0.0 copy-start.1
  0.7 0.0 copy-start.2
  0.7 0.0 copy-start.3
  0.7 0.0 copy-start.4
  0.7 2.0 %send.1 = (f32[16,256]{1,0:T(8,128)}, f32[128,128]{1,0:T(8,128)S(1)}, f32[40,2048]{1,0:T(8,128)S(1)}, f32[40,2048]{1,0:T(8,128)S(1)}) custom-call(f32[16,256]{1,0:T(8,128)} %precip.1, f32[16,256]{1,0:T(8,128)} %pet.1, f32[16,256]{1,0:T(8,128)} %soil_init.1, f32[16,256]{1,0:T(8,128)} %ksat.1, s32[16,256]{1,0:T(8,128)} %land_mask.1, s32[16,128]{1,0:T(8,128)} %bitcast.13, ...), custom_call_target="tpu_custom_call" | custom-call | tf_op jit(solution)/shard_map/send/pallas_call | solution.py:296
  2.7 4.6 %collective-permute-start = (f32[40,2048]{1,0:T(8,128)S(1)}, f32[40,2048]{1,0:T(8,128)S(1)}, u32[]{:S(2)}, u32[]{:S(2)}) collective-permute-start(f32[40,2048]{1,0:T(8,128)S(1)} %get-tuple-element.13), channel_id=1, source_target_pairs={{0,1},{1,2},{2,3},{3,4},{4,5},{5,6},{6,7},{7,8},{8,9},{9,10},{10,1... | collective-permute-start | bytes 983048 | tf_op jit(solution)/shard_map/ppermute | solution.py:324
  7.3 1.9 %collective-permute-start.1 = (f32[40,2048]{1,0:T(8,128)S(1)}, f32[40,2048]{1,0:T(8,128)S(1)}, u32[]{:S(2)}, u32[]{:S(2)}) collective-permute-start(f32[40,2048]{1,0:T(8,128)S(1)} %get-tuple-element.14), channel_id=1, source_target_pairs={{1,0},{2,1},{3,2},{4,3},{5,4},{6,5},{7,6},{8,7},{9,8},{10,9},{11,1... | collective-permute-start | bytes 983048 | tf_op jit(solution)/shard_map/ppermute | solution.py:325
  9.2 19.4 %all_to_all.16 = f32[32,4,128]{2,1,0:T(4,128)S(1)} all-to-all(f32[32,4,128]{2,1,0:T(4,128)S(1)} %bitcast.10), channel_id=1, replica_groups=mesh['member'=8,'tile'=32] {'tile'}, dimensions={0} | all-to-all | bytes 131072 | tf_op jit(solution)/shard_map/all_to_all | solution.py:326
  28.6 0.0 collective-permute-done.above
  28.6 0.0 collective-permute-done.1.below
  28.6 0.0 copy-done
  28.6 0.0 copy-done.1
  28.7 0.0 copy-done.2
  28.7 0.0 copy-done.3
  28.7 0.0 copy-done.4
  28.7 8.5 %route.1 = (f32[32,2048]{1,0:T(8,128)}, f32[32,2048]{1,0:T(8,128)}, f32[32,128]{1,0:T(8,128)S(1)}) custom-call(f32[128,128]{1,0:T(8,128)S(1)} %bitcast.8, f32[32,2048]{1,0:T(8,128)S(1)} %copy-done, f32[32,2048]{1,0:T(8,128)S(1)} %copy-done.1, f32[32,2048]{1,0:T(8,128)S(1)} %copy-done.2, f32[32,2048]{1,0:T(8,128)S(1)} %copy-done.3, s32[32,2048]{1,0:T(8,128)S(1)} %copy-done.4, ...), custom_call_target="tpu_custom_call" | custom-call | tf_op jit(solution)/shard_map/route/pallas_call | solution.py:332
  37.2 11.0 %all_to_all.17 = f32[32,1,128]{2,1,0:T(1,128)S(1)} all-to-all(f32[32,1,128]{2,1,0:T(1,128)S(1)} %bitcast.12), channel_id=1, replica_groups=mesh['member'=8,'tile'=32] {'tile'}, dimensions={0} | all-to-all | bytes 32768 | tf_op jit(solution)/shard_map/all_to_all | solution.py:348
  48.2 1.0 %reach_sums.1 = f32[16,128]{1,0:T(8,128)} custom-call(f32[128,128]{1,0:T(8,128)S(1)} %bitcast.9, f32[32,128]{1,0:T(8,128)S(1)} %bitcast.11), custom_call_target="tpu_custom_call" | custom-call | tf_op jit(solution)/shard_map/reach_sums/pallas_call | solution.py:349
Async XLA Ops:
  0.6 28.0 %copy-start = (f32[32,2048]{1,0:T(8,128)S(1)}, f32[32,2048]{1,0:T(8,128)}, u32[]{:S(2)}) copy-start(f32[32,2048]{1,0:T(8,128)} %head_init.1) | copy-start | bytes 786436
  0.6 28.0 %copy-start.1 = (f32[32,2048]{1,0:T(8,128)S(1)}, f32[32,2048]{1,0:T(8,128)}, u32[]{:S(2)}) copy-start(f32[32,2048]{1,0:T(8,128)} %sub_init.1) | copy-start | bytes 786436
  0.7 28.0 %copy-start.2 = (f32[32,2048]{1,0:T(8,128)S(1)}, f32[32,2048]{1,0:T(8,128)}, u32[]{:S(2)}) copy-start(f32[32,2048]{1,0:T(8,128)} %conduct.3) | copy-start | bytes 786436
  0.7 28.0 %copy-start.3 = (f32[32,2048]{1,0:T(8,128)S(1)}, f32[32,2048]{1,0:T(8,128)}, u32[]{:S(2)}) copy-start(f32[32,2048]{1,0:T(8,128)} %drain.3) | copy-start | bytes 786436
  0.7 28.0 %copy-start.4 = (s32[32,2048]{1,0:T(8,128)S(1)}, s32[32,2048]{1,0:T(8,128)}, u32[]{:S(2)}) copy-start(s32[32,2048]{1,0:T(8,128)} %code.3) | copy-start | bytes 786436
  2.7 25.9 %collective-permute-start = (f32[40,2048]{1,0:T(8,128)S(1)}, f32[40,2048]{1,0:T(8,128)S(1)}, u32[]{:S(2)}, u32[]{:S(2)}) collective-permute-start(f32[40,2048]{1,0:T(8,128)S(1)} %get-tuple-element.13), channel_id=1, source_target_pairs={{0,1},{1,2},{2,3},{3,4},{4,5},{5,6},{6,7},{7,8},{8,9},{9,10},{10,1... | collective-permute-start | bytes 983048 | tf_op jit(solution)/shard_map/ppermute | solution.py:324
  7.3 21.3 %collective-permute-start.1 = (f32[40,2048]{1,0:T(8,128)S(1)}, f32[40,2048]{1,0:T(8,128)S(1)}, u32[]{:S(2)}, u32[]{:S(2)}) collective-permute-start(f32[40,2048]{1,0:T(8,128)S(1)} %get-tuple-element.14), channel_id=1, source_target_pairs={{1,0},{2,1},{3,2},{4,3},{5,4},{6,5},{7,6},{8,7},{9,8},{10,9},{11,1... | collective-permute-start | bytes 983048 | tf_op jit(solution)/shard_map/ppermute | solution.py:325

commit v3 on v2

--- a/solution.py
+++ b/solution.py
@@ -38,29 +38,16 @@
     return jnp.where(iota(tile.shape, 1) == LANES - 1, after, tile)
 
 
-def send_kernel(
-    precip, pet, soil_init, ksat, land_mask, places, head, sub, conduct, drain, code,
-    soil_out, msg, top, bottom, turned, fields_in, mask_in, place_in, code_edge, sem,
+def land_kernel(
+    precip, pet, soil_init, ksat, land_mask, places,
+    soil_out, msg, turned, fields_in, mask_in, place_in, sem,
 ):
     local = []
     for i, ref in enumerate((precip, pet, soil_init, ksat)):
-        local.append(pltpu.make_async_copy(ref, fields_in.at[i], sem.at[10 + i]))
-    local.append(pltpu.make_async_copy(land_mask, mask_in, sem.at[14]))
-    local.append(pltpu.make_async_copy(places, place_in, sem.at[15]))
-    copies = []
-    for i, ref in enumerate((head, sub, conduct, drain)):
-        into = slice(8 * i, 8 * i + 8)
-        copies.append(pltpu.make_async_copy(ref.at[24:32, :], bottom.at[into, :], sem.at[2 * i]))
-        copies.append(pltpu.make_async_copy(ref.at[0:8, :], top.at[into, :], sem.at[2 * i + 1]))
-    codes = (
-        pltpu.make_async_copy(code.at[24:32, :], code_edge.at[0], sem.at[8]),
-        pltpu.make_async_copy(code.at[0:8, :], code_edge.at[1], sem.at[9]),
-    )
+        local.append(pltpu.make_async_copy(ref, fields_in.at[i], sem.at[i]))
+    local.append(pltpu.make_async_copy(land_mask, mask_in, sem.at[4]))
+    local.append(pltpu.make_async_copy(places, place_in, sem.at[5]))
     for c in local:
-        c.start()
-    for c in codes:
-        c.start()
-    for c in copies:
         c.start()
     for c in local:
         c.wait()
@@ -90,18 +77,51 @@
     place = place_in[...].astype(F32)
     msg[pl.ds(3, 16, stride=8), :] = place
     msg[pl.ds(7, 16, stride=8), :] = pltpu.roll(place, 64, 1)
-    for c in codes:
+
+
+def edge_kernel(head, sub, conduct, drain, code, top, bottom, code_edge, sem):
+    copies = []
+    for i, ref in enumerate((head, sub, conduct, drain, code)):
+        into = slice(HALO * i, HALO * i + HALO)
+        to_top = code_edge.at[0] if i == 4 else top.at[into, :]
+        to_bottom = code_edge.at[1] if i == 4 else bottom.at[into, :]
+        copies.append(pltpu.make_async_copy(ref.at[0:HALO, :], to_top, sem.at[2 * i]))
+        copies.append(
+            pltpu.make_async_copy(ref.at[OWN - HALO : OWN, :], to_bottom, sem.at[2 * i + 1])
+        )
+    for c in reversed(copies):
+        c.start()
+    for c in copies[8:]:
         c.wait()
-    bottom[32:40, :] = code_edge[0].astype(F32)
-    top[32:40, :] = code_edge[1].astype(F32)
-    for c in copies:
+    top[4 * HALO :, :] = code_edge[0].astype(F32)
+    bottom[4 * HALO :, :] = code_edge[1].astype(F32)
+    for c in copies[:8]:
         c.wait()
+
+
+def spread_kernel(land, head_init, sub_init, conduct, drain, code, fine_out, turned):
+    width = fine_out.shape[1]
+    data = jnp.concatenate([land[pl.ds(j, 32, stride=4), :] for j in range(3)], axis=1)
+    a, b, c = split3(data)
+    turned[...] = jnp.concatenate([a, b, c, jnp.zeros_like(a)], axis=0).T
+    lhs = jnp.concatenate([turned[pl.ds(q, 24, stride=16), :] for q in range(16)], axis=0)
+    lhs = lhs.astype(BF16)
+    src = iota((LANES, 256), 0)
+    dst = iota((LANES, 256), 1)
+    col = (iota((24, 256), 1) & 63) >> 2
+    for n in range(width // 256):
+        hot = ((src & 31) == ((dst + 256 * n) >> 6)) & (src < 96)
+        spread = jnp.dot(lhs, jnp.where(hot, 1.0, 0.0).astype(BF16), preferred_element_type=F32)
+        fine = spread[0:24]
+        for q in range(1, 16):
+            fine = jnp.where(col == q, spread[24 * q : 24 * q + 24], fine)
+        fine_out[:, 256 * n : 256 * n + 256] = fine
 
 
 def route_kernel(
     land, head_init, sub_init, conduct, drain, code, above, below, share, slot,
     head_out, sub_out, msg,
-    turned, h_a, h_b, s_a, s_b, g_w, a_w, dn_w, up_w, rt_w, lf_w, kp_w,
+    h_a, h_b, s_a, s_b, g_w, a_w, dn_w, up_w, rt_w, lf_w, kp_w,
     head, sub, shares, slots, parts, sem,
 ):
     tiles = g_w.shape[0]
@@ -135,21 +155,9 @@
         total = total + right_of(pltpu.roll(g, LANES - 1, 1), right)
         a_w[j] = 1.0 - g * total
 
-    data = jnp.concatenate([land[pl.ds(j, 32, stride=4), :] for j in range(3)], axis=1)
-    a, b, c = split3(data)
-    turned[...] = jnp.concatenate([a, b, c, jnp.zeros_like(a)], axis=0).T
-    lhs = jnp.concatenate([turned[pl.ds(q, 24, stride=16), :] for q in range(16)], axis=0)
-    lhs = lhs.astype(BF16)
     low_half = iota((8, 256), 0) < 4
-    src = iota((LANES, 256), 0)
-    dst = iota((LANES, 256), 1)
-    col = (iota((24, 256), 1) & 63) >> 2
     for n in range(width // 256):
-        hot = ((src & 31) == ((dst + 256 * n) >> 6)) & (src < 96)
-        spread = jnp.dot(lhs, jnp.where(hot, 1.0, 0.0).astype(BF16), preferred_element_type=F32)
-        fine = spread[0:24]
-        for q in range(1, 16):
-            fine = jnp.where(col == q, spread[24 * q : 24 * q + 24], fine)
+        fine = land[:, 256 * n : 256 * n + 256]
         for i in range(ROWS // 8):
             here = slice(8 * i, 8 * i + 8)
             at = slice(256 * n, 256 * n + 256)
@@ -293,32 +301,34 @@
     def array(*shape):
         return jax.ShapeDtypeStruct(shape, F32)
 
-    soil, msg, top, bottom = pl.pallas_call(
-        send_kernel,
-        out_shape=(
-            array(*precip.shape), array(4 * peers, LANES), array(40, width), array(40, width),
-        ),
-        in_specs=[far] * 11,
-        out_specs=(vmem,) * 4,
+    soil, msg = pl.pallas_call(
+        land_kernel,
+        out_shape=(array(*precip.shape), array(4 * peers, LANES)),
+        in_specs=[far] * 6,
+        out_specs=(vmem,) * 2,
         scratch_shapes=[
             pltpu.VMEM((precip.shape[1] + 16, LANES), F32),
             pltpu.VMEM((4,) + precip.shape, F32),
             pltpu.VMEM(precip.shape, jnp.int32),
             pltpu.VMEM((16, LANES), jnp.int32),
-            pltpu.VMEM((2, 8, width), jnp.int32),
-            pltpu.SemaphoreType.DMA((16,)),
+            pltpu.SemaphoreType.DMA((6,)),
         ],
         compiler_params=pltpu.CompilerParams(vmem_limit_bytes=6 * MIB),
-        name="send",
-    )(
-        *map(
-            hbm,
-            (
-                precip, pet, soil_init, ksat, land_mask, slot_reach.reshape(-1, LANES),
-                head_init, subsurface_init, conduct, drain_rate, flow_code,
-            ),
-        )
-    )
+        name="land_step",
+    )(*map(hbm, (precip, pet, soil_init, ksat, land_mask, slot_reach.reshape(-1, LANES))))
+    grid = (head_init, subsurface_init, conduct, drain_rate, flow_code)
+    top, bottom = pl.pallas_call(
+        edge_kernel,
+        out_shape=(array(5 * HALO, width),) * 2,
+        in_specs=[far] * 5,
+        out_specs=(vmem,) * 2,
+        scratch_shapes=[
+            pltpu.VMEM((2, HALO, width), jnp.int32),
+            pltpu.SemaphoreType.DMA((10,)),
+        ],
+        compiler_params=pltpu.CompilerParams(vmem_limit_bytes=6 * MIB),
+        name="edges",
+    )(*map(hbm, grid))
     up = [(i, i + 1) for i in range(peers - 1)]
     down = [(j, i) for i, j in up]
     above = lax.ppermute(bottom, "tile", up)
@@ -327,6 +337,17 @@
         msg.reshape(peers, 4, LANES), "tile", split_axis=0, concat_axis=0, tiled=True
     ).reshape(4 * peers, LANES)
 
+    fine = pl.pallas_call(
+        spread_kernel,
+        out_shape=array(24, width),
+        in_specs=[vmem] * 6,
+        out_specs=vmem,
+        scratch_shapes=[pltpu.VMEM((384, LANES), F32)],
+        compiler_params=pltpu.CompilerParams(vmem_limit_bytes=8 * MIB),
+        cost_estimate=pl.CostEstimate(flops=4*10**9, transcendentals=0, bytes_accessed=1 << 18),
+        name="spread",
+    )(land, *grid)
+
     window = pltpu.VMEM((tiles, ROWS, LANES), F32)
     plane = pltpu.VMEM((OWN, width), F32)
     head, sub, sums = pl.pallas_call(
@@ -334,17 +355,13 @@
         out_shape=(array(OWN, width), array(OWN, width), array(peers, LANES)),
         in_specs=[vmem] * 8 + [far] * 2,
         out_specs=(far, far, vmem),
-        scratch_shapes=[pltpu.VMEM((384, LANES), F32)]
-        + [window] * 11
+        scratch_shapes=[window] * 11
         + [plane] * 3
         + [pltpu.VMEM((OWN, width), jnp.int32), pltpu.VMEM((5, OWN, width), F32)]
         + [pltpu.SemaphoreType.DMA((4,))],
         compiler_params=pltpu.CompilerParams(vmem_limit_bytes=16 * MIB),
         name="route",
-    )(
-        land, head_init, subsurface_init, conduct, drain_rate, flow_code, above, below,
-        hbm(channel_share), hbm(cell_slot),
-    )
+    )(fine, *grid, above, below, hbm(channel_share), hbm(cell_slot))
     sums = lax.all_to_all(sums, "tile", split_axis=0, concat_axis=0, tiled=True)
     reach = pl.pallas_call(
         reach_kernel,

time: 49.4 us -> 51.7 us (1.047)
  blocking collectives: 30.4 us -> 16.7 us
  starting transfers between devices: 6.52 us -> 16.6 us
  waiting for transfers between devices: 0.01 us -> 5.73 us
    all_to_all x1 -> x0, blocking collectives: 19.4 us -> none  [local(): lax.all_to_all(msg.reshape(peers, 4, LANES), 'tile', split_axis=0, concat...]
    all_to_all x0 -> x1, starting transfers between devices: none -> 11.1 us  [local(): lax.all_to_all(msg.reshape(peers, 4, LANES), 'tile', split_axis=0, concat...]
    all_to_all x1, blocking collectives: 11 us -> 16.7 us  [local(): sums = lax.all_to_all(sums, 'tile', split_axis=0, concat_axis=0, tiled=True)]
    ppermute x1, waiting for transfers between devices: 0.01 us -> 4.25 us  [local(): below = lax.ppermute(top, 'tile', down)]
    pallas_call x1 -> x3, Pallas kernels: 2 us -> 3.59 us  [the longest x1 1.6 us: local(): pl.pallas_call(land_kernel, out_shape=(array(*precip.shape), array(4 * pe...]
    all_to_all x0 -> x1, waiting for transfers between devices: none -> 1.48 us  [local(): lax.all_to_all(msg.reshape(peers, 4, LANES), 'tile', split_axis=0, concat...]
    pallas_call x1, Pallas kernels: 8.46 us -> 6.98 us  [local(): pl.pallas_call(route_kernel, out_shape=(array(OWN, width), array(OWN, wid...]
    ppermute x1, starting transfers between devices: 4.59 us -> 3.54 us  [local(): above = lax.ppermute(bottom, 'tile', up)]
  transfers between devices with their start and end apart: 2 -> 3, of which waited for: 0 -> 2; matrix products, arithmetic and copies ran while one was open for 0% -> 0% of each run, Pallas kernels for 0% -> 4%
where the time goes in v3:
time: 51.7 us; the launch traced here: 51.3 us
  blocking collectives  16.7 us (32%)
  starting transfers between devices  16.6 us (32%)
  Pallas kernels  11.5 us (22%)
  waiting for transfers between devices  5.73 us (11%)
  between operations  0.75 us (1%)
    all_to_all x1, blocking collectives, local(): sums = lax.all_to_all(sums, 'tile', split_axis=0, concat_axis=0, tiled=True)  16.7 us
    all_to_all x1, starting transfers between devices, local(): lax.all_to_all(msg.reshape(peers, 4, LANES), 'tile', split_axis=0, concat...  11.1 us
    pallas_call x1, Pallas kernels, local(): pl.pallas_call(route_kernel, out_shape=(array(OWN, width), array(OWN, wid...  6.98 us
    ppermute x1, waiting for transfers between devices, local(): below = lax.ppermute(top, 'tile', down)  4.25 us
    ppermute x1, starting transfers between devices, local(): above = lax.ppermute(bottom, 'tile', up)  3.54 us
    ppermute x1, starting transfers between devices, local(): below = lax.ppermute(top, 'tile', down)  1.92 us
    pallas_call x1, Pallas kernels, local(): pl.pallas_call(land_kernel, out_shape=(array(*precip.shape), array(4 * pe...  1.6 us
    all_to_all x1, waiting for transfers between devices, local(): lax.all_to_all(msg.reshape(peers, 4, LANES), 'tile', split_axis=0, concat...  1.48 us
  transfers between devices with their start and end apart: 3, of which 2 were waited for; matrix products, arithmetic and copies ran while one was open for 0% of the time, Pallas kernels for 4%

profile of v3, /device:TPU:1, one launch (start us, length us, event | category | flops | bytes accessed | tf_op | source)
XLA Modules:
  0.0 51.3 jit_solution(15677576095167961878)
XLA Ops:
  0.6 1.6 %land_step.1 = (f32[16,256]{1,0:T(8,128)}, f32[128,128]{1,0:T(8,128)}) custom-call(f32[16,256]{1,0:T(8,128)} %precip.1, f32[16,256]{1,0:T(8,128)} %pet.1, f32[16,256]{1,0:T(8,128)} %soil_init.1, f32[16,256]{1,0:T(8,128)} %ksat.1, s32[16,256]{1,0:T(8,128)} %land_mask.1, s32[16,128]{1,0:T(8,128)} %bitcast.12), custom_call_target="tpu_custom_call" | custom-call | tf_op jit(solution)/shard_map/land_step/pallas_call | solution.py:304
  2.2 11.1 %all-to-all-start = ((f32[32,4,128]{2,1,0:T(4,128)}), f32[32,4,128]{2,1,0:T(4,128)S(1)}, u32[]{:S(2)}, u32[]{:S(2)}) async-start(f32[32,4,128]{2,1,0:T(4,128)} %bitcast.1), calls=%async_computation | async-start | bytes 131072 | tf_op jit(solution)/shard_map/all_to_all | solution.py:336
  13.4 0.0 copy-start
  13.4 0.0 copy-start.1
  13.4 0.0 copy-start.2
  13.4 0.0 copy-start.3
  13.4 0.0 copy-start.4
  13.5 1.3 %edges.1 = (f32[40,2048]{1,0:T(8,128)S(1)}, f32[40,2048]{1,0:T(8,128)S(1)}) custom-call(f32[32,2048]{1,0:T(8,128)} %head_init.3, f32[32,2048]{1,0:T(8,128)} %sub_init.3, f32[32,2048]{1,0:T(8,128)} %conduct.5, f32[32,2048]{1,0:T(8,128)} %drain.5, s32[32,2048]{1,0:T(8,128)} %code.5), custom_call_target="tpu_custom_call" | custom-call | tf_op jit(solution)/shard_map/edges/pallas_call | solution.py:320
  14.8 3.5 %collective-permute-start = (f32[40,2048]{1,0:T(8,128)S(1)}, f32[40,2048]{1,0:T(8,128)S(1)}, u32[]{:S(2)}, u32[]{:S(2)}) collective-permute-start(f32[40,2048]{1,0:T(8,128)S(1)} %get-tuple-element.13), channel_id=1, source_target_pairs={{0,1},{1,2},{2,3},{3,4},{4,5},{5,6},{6,7},{7,8},{8,9},{9,10},{10,1... | collective-permute-start | bytes 983048 | tf_op jit(solution)/shard_map/ppermute | solution.py:334
  18.3 1.9 %collective-permute-start.1 = (f32[40,2048]{1,0:T(8,128)S(1)}, f32[40,2048]{1,0:T(8,128)S(1)}, u32[]{:S(2)}, u32[]{:S(2)}) collective-permute-start(f32[40,2048]{1,0:T(8,128)S(1)} %get-tuple-element.14), channel_id=1, source_target_pairs={{1,0},{2,1},{3,2},{4,3},{5,4},{6,5},{7,6},{8,7},{9,8},{10,9},{11,1... | collective-permute-start | bytes 983048 | tf_op jit(solution)/shard_map/ppermute | solution.py:335
  20.2 1.5 %all-to-all-done = f32[32,4,128]{2,1,0:T(4,128)S(1)} async-done(((f32[32,4,128]{2,1,0:T(4,128)}), f32[32,4,128]{2,1,0:T(4,128)S(1)}, u32[]{:S(2)}, u32[]{:S(2)}) %all-to-all-start) | async-done | bytes 65568 | tf_op jit(solution)/shard_map/all_to_all | solution.py:336
  21.7 0.0 copy-done
  21.7 0.0 copy-done.1
  21.7 0.0 copy-done.2
  21.7 0.0 copy-done.3
  21.7 0.0 copy-done.4
  21.8 0.7 %spread.1.land = f32[24,2048]{1,0:T(8,128)S(1)} custom-call(f32[128,128]{1,0:T(8,128)S(1)} %bitcast.8, f32[32,2048]{1,0:T(8,128)S(1)} %copy-done, f32[32,2048]{1,0:T(8,128)S(1)} %copy-done.1, f32[32,2048]{1,0:T(8,128)S(1)} %copy-done.2, f32[32,2048]{1,0:T(8,128)S(1)} %copy-done.3, s32[32,2048]{1,0:T(8,128)S(1)} %copy-done.4), custom_call_target="tpu_custom_call" | custom-call | flops 4000000000 | bytes 262144 | tf_op jit(solution)/shard_map/spread/pallas_call | solution.py:340
  22.4 0.0 collective-permute-done.above
  22.5 4.2 %collective-permute-done.1.below = f32[40,2048]{1,0:T(8,128)S(1)} collective-permute-done((f32[40,2048]{1,0:T(8,128)S(1)}, f32[40,2048]{1,0:T(8,128)S(1)}, u32[]{:S(2)}, u32[]{:S(2)}) %collective-permute-start.1) | collective-permute-done | bytes 327712 | tf_op jit(solution)/shard_map/ppermute | solution.py:335
  26.7 7.0 %route.1 = (f32[32,2048]{1,0:T(8,128)}, f32[32,2048]{1,0:T(8,128)}, f32[32,128]{1,0:T(8,128)S(1)}) custom-call(f32[24,2048]{1,0:T(8,128)S(1)} %spread.1.land, f32[32,2048]{1,0:T(8,128)S(1)} %copy-done, f32[32,2048]{1,0:T(8,128)S(1)} %copy-done.1, f32[32,2048]{1,0:T(8,128)S(1)} %copy-done.2, f32[32,2048]{1,0:T(8,128)S(1)} %copy-done.3, ...), custom_call_target="tpu_custom_call" | custom-call | tf_op jit(solution)/shard_map/route/pallas_call | solution.py:353
  33.7 16.7 %all_to_all.16 = f32[32,1,128]{2,1,0:T(1,128)S(1)} all-to-all(f32[32,1,128]{2,1,0:T(1,128)S(1)} %bitcast.11), channel_id=1, replica_groups=mesh['member'=8,'tile'=32] {'tile'}, dimensions={0} | all-to-all | bytes 32768 | tf_op jit(solution)/shard_map/all_to_all | solution.py:365
  50.4 1.0 %reach_sums.1 = f32[16,128]{1,0:T(8,128)} custom-call(f32[128,128]{1,0:T(8,128)S(1)} %bitcast.9, f32[32,128]{1,0:T(8,128)S(1)} %bitcast.10), custom_call_target="tpu_custom_call" | custom-call | tf_op jit(solution)/shard_map/reach_sums/pallas_call | solution.py:366
Async XLA Ops:
  2.2 19.5 %all-to-all-start = ((f32[32,4,128]{2,1,0:T(4,128)}), f32[32,4,128]{2,1,0:T(4,128)S(1)}, u32[]{:S(2)}, u32[]{:S(2)}) async-start(f32[32,4,128]{2,1,0:T(4,128)} %bitcast.1), calls=%async_computation | async-start | bytes 131072 | tf_op jit(solution)/shard_map/all_to_all | solution.py:336
  13.4 8.3 %copy-start = (f32[32,2048]{1,0:T(8,128)S(1)}, f32[32,2048]{1,0:T(8,128)}, u32[]{:S(2)}) copy-start(f32[32,2048]{1,0:T(8,128)} %head_init.3) | copy-start | bytes 786436
  13.4 8.3 %copy-start.1 = (f32[32,2048]{1,0:T(8,128)S(1)}, f32[32,2048]{1,0:T(8,128)}, u32[]{:S(2)}) copy-start(f32[32,2048]{1,0:T(8,128)} %sub_init.3) | copy-start | bytes 786436
  13.4 8.3 %copy-start.2 = (f32[32,2048]{1,0:T(8,128)S(1)}, f32[32,2048]{1,0:T(8,128)}, u32[]{:S(2)}) copy-start(f32[32,2048]{1,0:T(8,128)} %conduct.5) | copy-start | bytes 786436
  13.4 8.3 %copy-start.3 = (f32[32,2048]{1,0:T(8,128)S(1)}, f32[32,2048]{1,0:T(8,128)}, u32[]{:S(2)}) copy-start(f32[32,2048]{1,0:T(8,128)} %drain.5) | copy-start | bytes 786436
  13.4 8.3 %copy-start.4 = (s32[32,2048]{1,0:T(8,128)S(1)}, s32[32,2048]{1,0:T(8,128)}, u32[]{:S(2)}) copy-start(s32[32,2048]{1,0:T(8,128)} %code.5) | copy-start | bytes 786436
  14.8 7.7 %collective-permute-start = (f32[40,2048]{1,0:T(8,128)S(1)}, f32[40,2048]{1,0:T(8,128)S(1)}, u32[]{:S(2)}, u32[]{:S(2)}) collective-permute-start(f32[40,2048]{1,0:T(8,128)S(1)} %get-tuple-element.13), channel_id=1, source_target_pairs={{0,1},{1,2},{2,3},{3,4},{4,5},{5,6},{6,7},{7,8},{8,9},{9,10},{10,1... | collective-permute-start | bytes 983048 | tf_op jit(solution)/shard_map/ppermute | solution.py:334
  18.3 8.4 %collective-permute-start.1 = (f32[40,2048]{1,0:T(8,128)S(1)}, f32[40,2048]{1,0:T(8,128)S(1)}, u32[]{:S(2)}, u32[]{:S(2)}) collective-permute-start(f32[40,2048]{1,0:T(8,128)S(1)} %get-tuple-element.14), channel_id=1, source_target_pairs={{1,0},{2,1},{3,2},{4,3},{5,4},{6,5},{7,6},{8,7},{9,8},{10,9},{11,1... | collective-permute-start | bytes 983048 | tf_op jit(solution)/shard_map/ppermute | solution.py:335

commit v4 on v2

--- a/solution.py
+++ b/solution.py
@@ -40,21 +40,24 @@
 
 def send_kernel(
     precip, pet, soil_init, ksat, land_mask, places, head, sub, conduct, drain, code,
-    soil_out, msg, top, bottom, turned, fields_in, mask_in, place_in, code_edge, sem,
+    soil_out, msg, near, far, turned, fields_in, mask_in, place_in, code_edge, sem,
 ):
     local = []
     for i, ref in enumerate((precip, pet, soil_init, ksat)):
         local.append(pltpu.make_async_copy(ref, fields_in.at[i], sem.at[10 + i]))
     local.append(pltpu.make_async_copy(land_mask, mask_in, sem.at[14]))
     local.append(pltpu.make_async_copy(places, place_in, sem.at[15]))
+    odd = lax.axis_index("tile") & 1
+    near_rows = pl.ds(pl.multiple_of((1 - odd) * (OWN - HALO), HALO), HALO)
+    far_rows = pl.ds(pl.multiple_of(odd * (OWN - HALO), HALO), HALO)
     copies = []
     for i, ref in enumerate((head, sub, conduct, drain)):
-        into = slice(8 * i, 8 * i + 8)
-        copies.append(pltpu.make_async_copy(ref.at[24:32, :], bottom.at[into, :], sem.at[2 * i]))
-        copies.append(pltpu.make_async_copy(ref.at[0:8, :], top.at[into, :], sem.at[2 * i + 1]))
+        into = slice(HALO * i, HALO * i + HALO)
+        copies.append(pltpu.make_async_copy(ref.at[near_rows, :], near.at[into, :], sem.at[2 * i]))
+        copies.append(pltpu.make_async_copy(ref.at[far_rows, :], far.at[into, :], sem.at[2 * i + 1]))
     codes = (
-        pltpu.make_async_copy(code.at[24:32, :], code_edge.at[0], sem.at[8]),
-        pltpu.make_async_copy(code.at[0:8, :], code_edge.at[1], sem.at[9]),
+        pltpu.make_async_copy(code.at[near_rows, :], code_edge.at[0], sem.at[8]),
+        pltpu.make_async_copy(code.at[far_rows, :], code_edge.at[1], sem.at[9]),
     )
     for c in local:
         c.start()
@@ -92,14 +95,14 @@
     msg[pl.ds(7, 16, stride=8), :] = pltpu.roll(place, 64, 1)
     for c in codes:
         c.wait()
-    bottom[32:40, :] = code_edge[0].astype(F32)
-    top[32:40, :] = code_edge[1].astype(F32)
+    near[4 * HALO :, :] = code_edge[0].astype(F32)
+    far[4 * HALO :, :] = code_edge[1].astype(F32)
     for c in copies:
         c.wait()
 
 
 def route_kernel(
-    land, head_init, sub_init, conduct, drain, code, above, below, share, slot,
+    land, head_init, sub_init, conduct, drain, code, near, far, share, slot,
     head_out, sub_out, msg,
     turned, h_a, h_b, s_a, s_b, g_w, a_w, dn_w, up_w, rt_w, lf_w, kp_w,
     head, sub, shares, slots, parts, sem,
@@ -112,11 +115,20 @@
     share_copy.start()
     slot_copy.start()
 
+    odd = (lax.axis_index("tile") & 1) == 1
+
+    def above(field, at):
+        rows = slice(HALO * field, HALO * field + HALO)
+        return jnp.where(odd, near[rows, at], far[rows, at])
+
+    def below(field, at):
+        rows = slice(HALO * field, HALO * field + HALO)
+        return jnp.where(odd, far[rows, at], near[rows, at])
+
     def window(own, field, j):
-        lo = 8 * field
         at = cut(j)
         return jnp.concatenate(
-            [above[lo : lo + 8, at], own[:, at].astype(F32), below[lo : lo + 8, at]], axis=0
+            [above(field, at), own[:, at].astype(F32), below(field, at)], axis=0
         )
 
     for j in range(tiles):
@@ -154,9 +166,9 @@
             here = slice(8 * i, 8 * i + 8)
             at = slice(256 * n, 256 * n + 256)
             if i == 0:
-                h0, s0 = above[0:8, at], above[8:16, at]
+                h0, s0 = above(0, at), above(1, at)
             elif i == ROWS // 8 - 1:
-                h0, s0 = below[0:8, at], below[8:16, at]
+                h0, s0 = below(0, at), below(1, at)
             else:
                 rows = slice(8 * i - 8, 8 * i)
                 h0, s0 = head_init[rows, at], sub_init[rows, at]
@@ -282,7 +294,7 @@
     slot_reach,
 ):
     vmem = pl.BlockSpec(memory_space=pltpu.VMEM)
-    far = pl.BlockSpec(memory_space=pltpu.HBM)
+    outside = pl.BlockSpec(memory_space=pltpu.HBM)
     peers = lax.axis_size("tile")
     width = head_init.shape[1]
     tiles = width // LANES
@@ -293,12 +305,12 @@
     def array(*shape):
         return jax.ShapeDtypeStruct(shape, F32)
 
-    soil, msg, top, bottom = pl.pallas_call(
+    soil, msg, near, far = pl.pallas_call(
         send_kernel,
         out_shape=(
             array(*precip.shape), array(4 * peers, LANES), array(40, width), array(40, width),
         ),
-        in_specs=[far] * 11,
+        in_specs=[outside] * 11,
         out_specs=(vmem,) * 4,
         scratch_shapes=[
             pltpu.VMEM((precip.shape[1] + 16, LANES), F32),
@@ -319,10 +331,8 @@
             ),
         )
     )
-    up = [(i, i + 1) for i in range(peers - 1)]
-    down = [(j, i) for i, j in up]
-    above = lax.ppermute(bottom, "tile", up)
-    below = lax.ppermute(top, "tile", down)
+    near = lax.ppermute(near, "tile", [(i, i ^ 1) for i in range(peers)])
+    far = lax.ppermute(far, "tile", [(i, ((i + 1) ^ 1) - 1) for i in range(1, peers - 1)])
     land = lax.all_to_all(
         msg.reshape(peers, 4, LANES), "tile", split_axis=0, concat_axis=0, tiled=True
     ).reshape(4 * peers, LANES)
@@ -332,8 +342,8 @@
     head, sub, sums = pl.pallas_call(
         route_kernel,
         out_shape=(array(OWN, width), array(OWN, width), array(peers, LANES)),
-        in_specs=[vmem] * 8 + [far] * 2,
-        out_specs=(far, far, vmem),
+        in_specs=[vmem] * 8 + [outside] * 2,
+        out_specs=(outside, outside, vmem),
         scratch_shapes=[pltpu.VMEM((384, LANES), F32)]
         + [window] * 11
         + [plane] * 3
@@ -342,7 +352,7 @@
         compiler_params=pltpu.CompilerParams(vmem_limit_bytes=16 * MIB),
         name="route",
     )(
-        land, head_init, subsurface_init, conduct, drain_rate, flow_code, above, below,
+        land, head_init, subsurface_init, conduct, drain_rate, flow_code, near, far,
         hbm(channel_share), hbm(cell_slot),
     )
     sums = lax.all_to_all(sums, "tile", split_axis=0, concat_axis=0, tiled=True)

time: 49.4 us -> 45.4 us (0.919)
  blocking collectives: 30.4 us -> 27.7 us
  starting transfers between devices: 6.52 us -> 5.24 us
    all_to_all x1, blocking collectives: 19.4 us -> 16.7 us  [local(): lax.all_to_all(msg.reshape(peers, 4, LANES), 'tile', split_axis=0, concat...]
    ppermute x2, starting transfers between devices: 6.52 us -> 5.24 us  [the longest x1 3.33 us: local(): near = lax.ppermute(near, 'tile', [(i, i ^ 1) for i in range(peers)])]
where the time goes in v4:
time: 45.4 us; the launch traced here: 45.2 us
  blocking collectives  27.7 us (61%)
  Pallas kernels  11.5 us (25%)
  starting transfers between devices  5.24 us (12%)
  between operations  0.74 us (2%)
    all_to_all x1, blocking collectives, local(): lax.all_to_all(msg.reshape(peers, 4, LANES), 'tile', split_axis=0, concat...  16.7 us
    all_to_all x1, blocking collectives, local(): sums = lax.all_to_all(sums, 'tile', split_axis=0, concat_axis=0, tiled=True)  11 us
    pallas_call x1, Pallas kernels, local(): pl.pallas_call(route_kernel, out_shape=(array(OWN, width), array(OWN, wid...  8.57 us
    ppermute x1, starting transfers between devices, local(): near = lax.ppermute(near, 'tile', [(i, i ^ 1) for i in range(peers)])  3.33 us
    pallas_call x1, Pallas kernels, local(): pl.pallas_call(send_kernel, out_shape=(array(*precip.shape), array(4 * pe...  2 us
    ppermute x1, starting transfers between devices, local(): lax.ppermute(far, 'tile', [(i, (i + 1 ^ 1) - 1) for i in range(1, peers -...  1.91 us
    pallas_call x1, Pallas kernels, local(): pl.pallas_call(reach_kernel, out_shape=array(16, LANES), in_specs=[vmem]...  0.96 us
  transfers between devices with their start and end apart: 2, of which 0 were waited for; matrix products, arithmetic and copies ran while one was open for 0% of the time, Pallas kernels for 0%

profile of v4, /device:TPU:1, one launch (start us, length us, event | category | flops | bytes accessed | tf_op | source)
XLA Modules:
  0.0 45.2 jit_solution(1533466959598017204)
XLA Ops:
  0.6 0.0 copy-start
  0.6 0.0 copy-start.1
  0.7 0.0 copy-start.2
  0.7 0.0 copy-start.3
  0.7 0.0 copy-start.4
  0.7 2.0 %send.1 = (f32[16,256]{1,0:T(8,128)}, f32[128,128]{1,0:T(8,128)S(1)}, f32[40,2048]{1,0:T(8,128)S(1)}, f32[40,2048]{1,0:T(8,128)S(1)}) custom-call(f32[16,256]{1,0:T(8,128)} %precip.1, f32[16,256]{1,0:T(8,128)} %pet.1, f32[16,256]{1,0:T(8,128)} %soil_init.1, f32[16,256]{1,0:T(8,128)} %ksat.1, s32[16,256]{1,0:T(8,128)} %land_mask.1, s32[16,128]{1,0:T(8,128)} %bitcast.13, ...), custom_call_target="tpu_custom_call" | custom-call | tf_op jit(solution)/shard_map/send/pallas_call | solution.py:308
  2.7 3.3 %collective-permute-start = (f32[40,2048]{1,0:T(8,128)S(1)}, f32[40,2048]{1,0:T(8,128)S(1)}, u32[]{:S(2)}, u32[]{:S(2)}) collective-permute-start(f32[40,2048]{1,0:T(8,128)S(1)} %get-tuple-element.13), channel_id=1, source_target_pairs={{0,1},{1,0},{2,3},{3,2},{4,5},{5,4},{6,7},{7,6},{8,9},{9,8},{10,11... | collective-permute-start | bytes 983048 | tf_op jit(solution)/shard_map/ppermute | solution.py:334
  6.0 1.9 %collective-permute-start.1 = (f32[40,2048]{1,0:T(8,128)S(1)}, f32[40,2048]{1,0:T(8,128)S(1)}, u32[]{:S(2)}, u32[]{:S(2)}) collective-permute-start(f32[40,2048]{1,0:T(8,128)S(1)} %get-tuple-element.14), channel_id=1, source_target_pairs={{1,2},{2,1},{3,4},{4,3},{5,6},{6,5},{7,8},{8,7},{9,10},{10,9},{11,... | collective-permute-start | bytes 983048 | tf_op jit(solution)/shard_map/ppermute | solution.py:335
  7.9 16.7 %all_to_all.16 = f32[32,4,128]{2,1,0:T(4,128)S(1)} all-to-all(f32[32,4,128]{2,1,0:T(4,128)S(1)} %bitcast.10), channel_id=1, replica_groups=mesh['member'=8,'tile'=32] {'tile'}, dimensions={0} | all-to-all | bytes 131072 | tf_op jit(solution)/shard_map/all_to_all | solution.py:336
  24.6 0.0 collective-permute-done.near
  24.6 0.0 collective-permute-done.1.far
  24.6 0.0 copy-done
  24.6 0.0 copy-done.1
  24.7 0.0 copy-done.2
  24.7 0.0 copy-done.3
  24.7 0.0 copy-done.4
  24.7 8.6 %route.1 = (f32[32,2048]{1,0:T(8,128)}, f32[32,2048]{1,0:T(8,128)}, f32[32,128]{1,0:T(8,128)S(1)}) custom-call(f32[128,128]{1,0:T(8,128)S(1)} %bitcast.8, f32[32,2048]{1,0:T(8,128)S(1)} %copy-done, f32[32,2048]{1,0:T(8,128)S(1)} %copy-done.1, f32[32,2048]{1,0:T(8,128)S(1)} %copy-done.2, f32[32,2048]{1,0:T(8,128)S(1)} %copy-done.3, s32[32,2048]{1,0:T(8,128)S(1)} %copy-done.4, ...), custom_call_target="tpu_custom_call" | custom-call | tf_op jit(solution)/shard_map/route/pallas_call | solution.py:342
  33.3 11.0 %all_to_all.17 = f32[32,1,128]{2,1,0:T(1,128)S(1)} all-to-all(f32[32,1,128]{2,1,0:T(1,128)S(1)} %bitcast.12), channel_id=1, replica_groups=mesh['member'=8,'tile'=32] {'tile'}, dimensions={0} | all-to-all | bytes 32768 | tf_op jit(solution)/shard_map/all_to_all | solution.py:358
  44.3 1.0 %reach_sums.1 = f32[16,128]{1,0:T(8,128)} custom-call(f32[128,128]{1,0:T(8,128)S(1)} %bitcast.9, f32[32,128]{1,0:T(8,128)S(1)} %bitcast.11), custom_call_target="tpu_custom_call" | custom-call | tf_op jit(solution)/shard_map/reach_sums/pallas_call | solution.py:359
Async XLA Ops:
  0.6 24.0 %copy-start = (f32[32,2048]{1,0:T(8,128)S(1)}, f32[32,2048]{1,0:T(8,128)}, u32[]{:S(2)}) copy-start(f32[32,2048]{1,0:T(8,128)} %head_init.1) | copy-start | bytes 786436
  0.6 24.0 %copy-start.1 = (f32[32,2048]{1,0:T(8,128)S(1)}, f32[32,2048]{1,0:T(8,128)}, u32[]{:S(2)}) copy-start(f32[32,2048]{1,0:T(8,128)} %sub_init.1) | copy-start | bytes 786436
  0.7 24.0 %copy-start.2 = (f32[32,2048]{1,0:T(8,128)S(1)}, f32[32,2048]{1,0:T(8,128)}, u32[]{:S(2)}) copy-start(f32[32,2048]{1,0:T(8,128)} %conduct.3) | copy-start | bytes 786436
  0.7 24.0 %copy-start.3 = (f32[32,2048]{1,0:T(8,128)S(1)}, f32[32,2048]{1,0:T(8,128)}, u32[]{:S(2)}) copy-start(f32[32,2048]{1,0:T(8,128)} %drain.3) | copy-start | bytes 786436
  0.7 24.0 %copy-start.4 = (s32[32,2048]{1,0:T(8,128)S(1)}, s32[32,2048]{1,0:T(8,128)}, u32[]{:S(2)}) copy-start(s32[32,2048]{1,0:T(8,128)} %code.3) | copy-start | bytes 786436
  2.7 21.9 %collective-permute-start = (f32[40,2048]{1,0:T(8,128)S(1)}, f32[40,2048]{1,0:T(8,128)S(1)}, u32[]{:S(2)}, u32[]{:S(2)}) collective-permute-start(f32[40,2048]{1,0:T(8,128)S(1)} %get-tuple-element.13), channel_id=1, source_target_pairs={{0,1},{1,0},{2,3},{3,2},{4,5},{5,4},{6,7},{7,6},{8,9},{9,8},{10,11... | collective-permute-start | bytes 983048 | tf_op jit(solution)/shard_map/ppermute | solution.py:334
  6.0 18.6 %collective-permute-start.1 = (f32[40,2048]{1,0:T(8,128)S(1)}, f32[40,2048]{1,0:T(8,128)S(1)}, u32[]{:S(2)}, u32[]{:S(2)}) collective-permute-start(f32[40,2048]{1,0:T(8,128)S(1)} %get-tuple-element.14), channel_id=1, source_target_pairs={{1,2},{2,1},{3,4},{4,3},{5,6},{6,5},{7,8},{8,7},{9,10},{10,9},{11,... | collective-permute-start | bytes 983048 | tf_op jit(solution)/shard_map/ppermute | solution.py:335

commit v5 on v4

--- a/solution.py
+++ b/solution.py
@@ -191,7 +191,7 @@
             pltpu.roll(lf_w[j] * s, LANES - 1, 1),
         )
 
-    def substep(h_in, s_in, h_to, s_to):
+    def substep(h_in, s_in, keep, take):
         before = (zero,) * 5
         now = products(0, h_in, s_in)
         for j in range(tiles):
@@ -201,29 +201,40 @@
             flux = pltpu.roll(p, 1, 0) + pltpu.roll(p, ROWS - 1, 0)
             flux = flux + left_of(now[1], before[1])
             flux = flux + right_of(now[2], after[2])
-            h_to[j] = a_w[j] * h_in[j] + g_w[j] * flux
             new = pltpu.roll(dn_w[j] * s, 1, 0) + pltpu.roll(up_w[j] * s, ROWS - 1, 0)
-            new = new + kp_w[j] * s
             new = new + left_of(now[3], before[3])
-            s_to[j] = new + right_of(now[4], after[4])
+            new = new + right_of(now[4], after[4])
+            h = a_w[j, keep, :] * h_in[j, keep, :] + g_w[j, keep, :] * flux[keep]
+            take(j, h, new[keep] + kp_w[j, keep, :] * s[keep])
             before, now = now, after
 
-    for i in range(ITERS // 2):
-        substep(h_a, s_a, h_b, s_b)
-        substep(h_b, s_b, h_a, s_a)
-
+    def store(h_to, s_to):
+        def take(j, h, s):
+            h_to[j] = h
+            s_to[j] = s
+
+        return take
+
+    def finish(j, h, s):
+        at = cut(j)
+        sub[:, at] = s
+        inflow = shares[:, at] * h
+        head[:, at] = h - inflow
+        coarse = inflow.astype(BF16).astype(F32)
+        parts[0, :, at] = coarse
+        parts[1, :, at] = inflow - coarse
+        q = slots[:, at]
+        parts[2, :, at] = (q >> 6).astype(F32)
+        parts[3, :, at] = (q & 63).astype(F32)
+
+    source = (h_a, s_a)
+    target = (h_b, s_b)
+    for i in range(ITERS - 1):
+        substep(*source, slice(0, ROWS), store(*target))
+        source, target = target, source
     share_copy.wait()
     slot_copy.wait()
-    for j in range(tiles):
-        at = cut(j)
-        h = h_a[j, HALO : HALO + OWN, :]
-        sub[:, at] = s_a[j, HALO : HALO + OWN, :]
-        inflow = shares[:, at] * h
-        head[:, at] = h - inflow
-        parts[0, :, at], parts[1, :, at], parts[2, :, at] = split3(inflow)
-        q = slots[:, at]
-        parts[3, :, at] = (q >> 6).astype(F32)
-        parts[4, :, at] = (q & 63).astype(F32)
+    substep(*source, slice(HALO, HALO + OWN), finish)
     head_copy = pltpu.make_async_copy(head, head_out, sem.at[1])
     sub_copy = pltpu.make_async_copy(sub, sub_out, sem.at[2])
     head_copy.start()
@@ -232,24 +243,20 @@
     owner = iota((32, width), 0).astype(F32).astype(BF16)
     place = iota((64, width), 0).astype(F32).astype(BF16)
     one = jnp.ones((64, width), BF16)
-    none64 = jnp.zeros((64, width), BF16)
-    none32 = jnp.zeros((32, width), BF16)
-
-    def wide(row, n):
-        return jnp.broadcast_to(row, (n, width)).astype(BF16)
-
-    total = jnp.zeros((96, 64), F32)
+    none = jnp.zeros((64, width), BF16)
+
+    def wide(i, r, n):
+        return jnp.broadcast_to(parts[i, r : r + 1, :], (n, width)).astype(BF16)
+
+    total = jnp.zeros((64, 64), F32)
     for r in range(OWN):
-        at = slice(r, r + 1)
-        hi = wide(parts[3, at, :], 32) == owner
-        lhs = jnp.concatenate(
-            [jnp.where(hi, wide(parts[i, at, :], 32), none32) for i in range(3)], axis=0
-        )
-        rhs = jnp.where(wide(parts[4, at, :], 64) == place, one, none64)
+        hi = wide(2, r, 32) == owner
+        lhs = jnp.concatenate([jnp.where(hi, wide(i, r, 32), none[0:32]) for i in range(2)], axis=0)
+        rhs = jnp.where(wide(3, r, 64) == place, one, none)
         total = total + lax.dot_general(
             lhs, rhs, (((1,), (1,)), ((), ())), preferred_element_type=F32
         )
-    total = total[0:32] + total[32:64] + total[64:96]
+    total = total[0:32] + total[32:64]
     msg[...] = jnp.concatenate([total, jnp.zeros_like(total)], axis=1)
     head_copy.wait()
     sub_copy.wait()
@@ -347,7 +354,7 @@
         scratch_shapes=[pltpu.VMEM((384, LANES), F32)]
         + [window] * 11
         + [plane] * 3
-        + [pltpu.VMEM((OWN, width), jnp.int32), pltpu.VMEM((5, OWN, width), F32)]
+        + [pltpu.VMEM((OWN, width), jnp.int32), pltpu.VMEM((4, OWN, width), F32)]
         + [pltpu.SemaphoreType.DMA((4,))],
         compiler_params=pltpu.CompilerParams(vmem_limit_bytes=16 * MIB),
         name="route",

time: 45.4 us -> 43.8 us (0.965)
  Pallas kernels: 11.5 us -> 9.89 us
    pallas_call x1, Pallas kernels: 8.57 us -> 6.92 us  [local(): pl.pallas_call(route_kernel, out_shape=(array(OWN, width), array(OWN, wid...]
where the time goes in v5:
time: 43.8 us; the launch traced here: 43.6 us
  blocking collectives  27.7 us (63%)
  Pallas kernels  9.89 us (23%)
  starting transfers between devices  5.24 us (12%)
  between operations  0.74 us (2%)
    all_to_all x1, blocking collectives, local(): lax.all_to_all(msg.reshape(peers, 4, LANES), 'tile', split_axis=0, concat...  16.7 us
    all_to_all x1, blocking collectives, local(): sums = lax.all_to_all(sums, 'tile', split_axis=0, concat_axis=0, tiled=True)  11 us
    pallas_call x1, Pallas kernels, local(): pl.pallas_call(route_kernel, out_shape=(array(OWN, width), array(OWN, wid...  6.92 us
    ppermute x1, starting transfers between devices, local(): near = lax.ppermute(near, 'tile', [(i, i ^ 1) for i in range(peers)])  3.33 us
    pallas_call x1, Pallas kernels, local(): pl.pallas_call(send_kernel, out_shape=(array(*precip.shape), array(4 * pe...  2 us
    ppermute x1, starting transfers between devices, local(): lax.ppermute(far, 'tile', [(i, (i + 1 ^ 1) - 1) for i in range(1, peers -...  1.91 us
    pallas_call x1, Pallas kernels, local(): pl.pallas_call(reach_kernel, out_shape=array(16, LANES), in_specs=[vmem]...  0.96 us
  transfers between devices with their start and end apart: 2, of which 0 were waited for; matrix products, arithmetic and copies ran while one was open for 0% of the time, Pallas kernels for 0%

profile of v5, /device:TPU:1, one launch (start us, length us, event | category | flops | bytes accessed | tf_op | source)
XLA Modules:
  0.0 43.6 jit_solution(12638046325526113735)
XLA Ops:
  0.6 0.0 copy-start
  0.6 0.0 copy-start.1
  0.7 0.0 copy-start.2
  0.7 0.0 copy-start.3
  0.7 0.0 copy-start.4
  0.7 2.0 %send.1 = (f32[16,256]{1,0:T(8,128)}, f32[128,128]{1,0:T(8,128)S(1)}, f32[40,2048]{1,0:T(8,128)S(1)}, f32[40,2048]{1,0:T(8,128)S(1)}) custom-call(f32[16,256]{1,0:T(8,128)} %precip.1, f32[16,256]{1,0:T(8,128)} %pet.1, f32[16,256]{1,0:T(8,128)} %soil_init.1, f32[16,256]{1,0:T(8,128)} %ksat.1, s32[16,256]{1,0:T(8,128)} %land_mask.1, s32[16,128]{1,0:T(8,128)} %bitcast.13, ...), custom_call_target="tpu_custom_call" | custom-call | tf_op jit(solution)/shard_map/send/pallas_call | solution.py:315
  2.7 3.3 %collective-permute-start = (f32[40,2048]{1,0:T(8,128)S(1)}, f32[40,2048]{1,0:T(8,128)S(1)}, u32[]{:S(2)}, u32[]{:S(2)}) collective-permute-start(f32[40,2048]{1,0:T(8,128)S(1)} %get-tuple-element.13), channel_id=1, source_target_pairs={{0,1},{1,0},{2,3},{3,2},{4,5},{5,4},{6,7},{7,6},{8,9},{9,8},{10,11... | collective-permute-start | bytes 983048 | tf_op jit(solution)/shard_map/ppermute | solution.py:341
  6.0 1.9 %collective-permute-start.1 = (f32[40,2048]{1,0:T(8,128)S(1)}, f32[40,2048]{1,0:T(8,128)S(1)}, u32[]{:S(2)}, u32[]{:S(2)}) collective-permute-start(f32[40,2048]{1,0:T(8,128)S(1)} %get-tuple-element.14), channel_id=1, source_target_pairs={{1,2},{2,1},{3,4},{4,3},{5,6},{6,5},{7,8},{8,7},{9,10},{10,9},{11,... | collective-permute-start | bytes 983048 | tf_op jit(solution)/shard_map/ppermute | solution.py:342
  7.9 16.7 %all_to_all.16 = f32[32,4,128]{2,1,0:T(4,128)S(1)} all-to-all(f32[32,4,128]{2,1,0:T(4,128)S(1)} %bitcast.10), channel_id=1, replica_groups=mesh['member'=8,'tile'=32] {'tile'}, dimensions={0} | all-to-all | bytes 131072 | tf_op jit(solution)/shard_map/all_to_all | solution.py:343
  24.6 0.0 collective-permute-done.near
  24.6 0.0 collective-permute-done.1.far
  24.6 0.0 copy-done
  24.6 0.0 copy-done.1
  24.7 0.0 copy-done.2
  24.7 0.0 copy-done.3
  24.7 0.0 copy-done.4
  24.7 6.9 %route.1 = (f32[32,2048]{1,0:T(8,128)}, f32[32,2048]{1,0:T(8,128)}, f32[32,128]{1,0:T(8,128)S(1)}) custom-call(f32[128,128]{1,0:T(8,128)S(1)} %bitcast.8, f32[32,2048]{1,0:T(8,128)S(1)} %copy-done, f32[32,2048]{1,0:T(8,128)S(1)} %copy-done.1, f32[32,2048]{1,0:T(8,128)S(1)} %copy-done.2, f32[32,2048]{1,0:T(8,128)S(1)} %copy-done.3, s32[32,2048]{1,0:T(8,128)S(1)} %copy-done.4, ...), custom_call_target="tpu_custom_call" | custom-call | tf_op jit(solution)/shard_map/route/pallas_call | solution.py:349
  31.6 11.0 %all_to_all.17 = f32[32,1,128]{2,1,0:T(1,128)S(1)} all-to-all(f32[32,1,128]{2,1,0:T(1,128)S(1)} %bitcast.12), channel_id=1, replica_groups=mesh['member'=8,'tile'=32] {'tile'}, dimensions={0} | all-to-all | bytes 32768 | tf_op jit(solution)/shard_map/all_to_all | solution.py:365
  42.6 1.0 %reach_sums.1 = f32[16,128]{1,0:T(8,128)} custom-call(f32[128,128]{1,0:T(8,128)S(1)} %bitcast.9, f32[32,128]{1,0:T(8,128)S(1)} %bitcast.11), custom_call_target="tpu_custom_call" | custom-call | tf_op jit(solution)/shard_map/reach_sums/pallas_call | solution.py:366
Async XLA Ops:
  0.6 24.0 %copy-start = (f32[32,2048]{1,0:T(8,128)S(1)}, f32[32,2048]{1,0:T(8,128)}, u32[]{:S(2)}) copy-start(f32[32,2048]{1,0:T(8,128)} %head_init.1) | copy-start | bytes 786436
  0.6 24.0 %copy-start.1 = (f32[32,2048]{1,0:T(8,128)S(1)}, f32[32,2048]{1,0:T(8,128)}, u32[]{:S(2)}) copy-start(f32[32,2048]{1,0:T(8,128)} %sub_init.1) | copy-start | bytes 786436
  0.7 24.0 %copy-start.2 = (f32[32,2048]{1,0:T(8,128)S(1)}, f32[32,2048]{1,0:T(8,128)}, u32[]{:S(2)}) copy-start(f32[32,2048]{1,0:T(8,128)} %conduct.3) | copy-start | bytes 786436
  0.7 24.0 %copy-start.3 = (f32[32,2048]{1,0:T(8,128)S(1)}, f32[32,2048]{1,0:T(8,128)}, u32[]{:S(2)}) copy-start(f32[32,2048]{1,0:T(8,128)} %drain.3) | copy-start | bytes 786436
  0.7 24.0 %copy-start.4 = (s32[32,2048]{1,0:T(8,128)S(1)}, s32[32,2048]{1,0:T(8,128)}, u32[]{:S(2)}) copy-start(s32[32,2048]{1,0:T(8,128)} %code.3) | copy-start | bytes 786436
  2.7 21.9 %collective-permute-start = (f32[40,2048]{1,0:T(8,128)S(1)}, f32[40,2048]{1,0:T(8,128)S(1)}, u32[]{:S(2)}, u32[]{:S(2)}) collective-permute-start(f32[40,2048]{1,0:T(8,128)S(1)} %get-tuple-element.13), channel_id=1, source_target_pairs={{0,1},{1,0},{2,3},{3,2},{4,5},{5,4},{6,7},{7,6},{8,9},{9,8},{10,11... | collective-permute-start | bytes 983048 | tf_op jit(solution)/shard_map/ppermute | solution.py:341
  6.0 18.6 %collective-permute-start.1 = (f32[40,2048]{1,0:T(8,128)S(1)}, f32[40,2048]{1,0:T(8,128)S(1)}, u32[]{:S(2)}, u32[]{:S(2)}) collective-permute-start(f32[40,2048]{1,0:T(8,128)S(1)} %get-tuple-element.14), channel_id=1, source_target_pairs={{1,2},{2,1},{3,4},{4,3},{5,6},{6,5},{7,8},{8,7},{9,10},{10,9},{11,... | collective-permute-start | bytes 983048 | tf_op jit(solution)/shard_map/ppermute | solution.py:342

commit v6 on v5

--- a/solution.py
+++ b/solution.py
@@ -38,12 +38,19 @@
     return jnp.where(iota(tile.shape, 1) == LANES - 1, after, tile)
 
 
+def water(p, s0, k, mask):
+    wet = 2.0 * s0
+    cap = k * (1.0 - wet)
+    wet2 = wet * wet
+    return mask * p * p / (p + cap), 0.25 * mask * k * (wet2 * wet2)
+
+
 def send_kernel(
-    precip, pet, soil_init, ksat, land_mask, places, head, sub, conduct, drain, code,
-    soil_out, msg, near, far, turned, fields_in, mask_in, place_in, code_edge, sem,
+    precip, soil_init, ksat, land_mask, places, head, sub, conduct, drain, code,
+    msg, near, far, turned, fields_in, mask_in, place_in, code_edge, sem,
 ):
     local = []
-    for i, ref in enumerate((precip, pet, soil_init, ksat)):
+    for i, ref in enumerate((precip, soil_init, ksat)):
         local.append(pltpu.make_async_copy(ref, fields_in.at[i], sem.at[10 + i]))
     local.append(pltpu.make_async_copy(land_mask, mask_in, sem.at[14]))
     local.append(pltpu.make_async_copy(places, place_in, sem.at[15]))
@@ -67,17 +74,8 @@
         c.start()
     for c in local:
         c.wait()
-    mask = mask_in[...].astype(F32)
     p = fields_in[0]
-    s0 = fields_in[2]
-    k = fields_in[3]
-    wet = 2.0 * s0
-    cap = k * (1.0 - wet)
-    runoff = mask * p * p / (p + cap)
-    wet2 = wet * wet
-    drainage = 0.25 * mask * k * (wet2 * wet2)
-    evap = mask * fields_in[1] * wet
-    soil_out[...] = s0 + 0.1 * (mask * p - runoff - drainage - evap)
+    runoff, drainage = water(p, fields_in[1], fields_in[2], mask_in[...].astype(F32))
     rows = p.shape[1]
     fields = jnp.concatenate([runoff, drainage], axis=0)
     turned[0:8, :] = jnp.zeros((8, LANES), F32)
@@ -103,17 +101,23 @@
 
 def route_kernel(
     land, head_init, sub_init, conduct, drain, code, near, far, share, slot,
-    head_out, sub_out, msg,
+    precip, pet, soil_init, ksat, land_mask,
+    head_out, sub_out, msg, soil_out,
     turned, h_a, h_b, s_a, s_b, g_w, a_w, dn_w, up_w, rt_w, lf_w, kp_w,
-    head, sub, shares, slots, parts, sem,
+    head, sub, shares, slots, parts, fields_in, mask_in, soil, sem,
 ):
     tiles = g_w.shape[0]
     width = tiles * LANES
     zero = jnp.zeros((ROWS, LANES), F32)
     share_copy = pltpu.make_async_copy(share, shares, sem.at[0])
     slot_copy = pltpu.make_async_copy(slot, slots, sem.at[3])
+    local = [pltpu.make_async_copy(land_mask, mask_in, sem.at[8])]
+    for i, ref in enumerate((precip, pet, soil_init, ksat)):
+        local.append(pltpu.make_async_copy(ref, fields_in.at[i], sem.at[4 + i]))
     share_copy.start()
     slot_copy.start()
+    for c in local:
+        c.start()
 
     odd = (lax.axis_index("tile") & 1) == 1
 
@@ -232,6 +236,15 @@
     for i in range(ITERS - 1):
         substep(*source, slice(0, ROWS), store(*target))
         source, target = target, source
+    for c in local:
+        c.wait()
+    mask = mask_in[...].astype(F32)
+    p, s0 = fields_in[0], fields_in[2]
+    runoff, drainage = water(p, s0, fields_in[3], mask)
+    evap = mask * fields_in[1] * (2.0 * s0)
+    soil[...] = s0 + 0.1 * (mask * p - runoff - drainage - evap)
+    soil_copy = pltpu.make_async_copy(soil, soil_out, sem.at[9])
+    soil_copy.start()
     share_copy.wait()
     slot_copy.wait()
     substep(*source, slice(HALO, HALO + OWN), finish)
@@ -258,6 +271,7 @@
         )
     total = total[0:32] + total[32:64]
     msg[...] = jnp.concatenate([total, jnp.zeros_like(total)], axis=1)
+    soil_copy.wait()
     head_copy.wait()
     sub_copy.wait()
 
@@ -312,16 +326,16 @@
     def array(*shape):
         return jax.ShapeDtypeStruct(shape, F32)
 
-    soil, msg, near, far = pl.pallas_call(
+    msg, near, far = pl.pallas_call(
         send_kernel,
         out_shape=(
-            array(*precip.shape), array(4 * peers, LANES), array(40, width), array(40, width),
+            array(4 * peers, LANES), array(40, width), array(40, width),
         ),
-        in_specs=[outside] * 11,
-        out_specs=(vmem,) * 4,
+        in_specs=[outside] * 10,
+        out_specs=(vmem,) * 3,
         scratch_shapes=[
             pltpu.VMEM((precip.shape[1] + 16, LANES), F32),
-            pltpu.VMEM((4,) + precip.shape, F32),
+            pltpu.VMEM((3,) + precip.shape, F32),
             pltpu.VMEM(precip.shape, jnp.int32),
             pltpu.VMEM((16, LANES), jnp.int32),
             pltpu.VMEM((2, 8, width), jnp.int32),
@@ -333,7 +347,7 @@
         *map(
             hbm,
             (
-                precip, pet, soil_init, ksat, land_mask, slot_reach.reshape(-1, LANES),
+                precip, soil_init, ksat, land_mask, slot_reach.reshape(-1, LANES),
                 head_init, subsurface_init, conduct, drain_rate, flow_code,
             ),
         )
@@ -346,21 +360,24 @@
 
     window = pltpu.VMEM((tiles, ROWS, LANES), F32)
     plane = pltpu.VMEM((OWN, width), F32)
-    head, sub, sums = pl.pallas_call(
+    head, sub, sums, soil = pl.pallas_call(
         route_kernel,
-        out_shape=(array(OWN, width), array(OWN, width), array(peers, LANES)),
-        in_specs=[vmem] * 8 + [outside] * 2,
-        out_specs=(outside, outside, vmem),
+        out_shape=(
+            array(OWN, width), array(OWN, width), array(peers, LANES), array(*precip.shape),
+        ),
+        in_specs=[vmem] * 8 + [outside] * 7,
+        out_specs=(outside, outside, vmem, outside),
         scratch_shapes=[pltpu.VMEM((384, LANES), F32)]
         + [window] * 11
         + [plane] * 3
         + [pltpu.VMEM((OWN, width), jnp.int32), pltpu.VMEM((4, OWN, width), F32)]
-        + [pltpu.SemaphoreType.DMA((4,))],
+        + [pltpu.VMEM((4,) + precip.shape, F32), pltpu.VMEM(precip.shape, jnp.int32)]
+        + [pltpu.VMEM(precip.shape, F32), pltpu.SemaphoreType.DMA((10,))],
         compiler_params=pltpu.CompilerParams(vmem_limit_bytes=16 * MIB),
         name="route",
     )(
         land, head_init, subsurface_init, conduct, drain_rate, flow_code, near, far,
-        hbm(channel_share), hbm(cell_slot),
+        *map(hbm, (channel_share, cell_slot, precip, pet, soil_init, ksat, land_mask)),
     )
     sums = lax.all_to_all(sums, "tile", split_axis=0, concat_axis=0, tiled=True)
     reach = pl.pallas_call(

time: 43.8 us -> 43.3 us (0.989)
  Pallas kernels: 9.89 us -> 9.37 us
    pallas_call x1, Pallas kernels: 2 us -> 1.4 us  [local(): pl.pallas_call(send_kernel, out_shape=(array(4 * peers, LANES), array(40,...]
where the time goes in v6:
time: 43.3 us; the launch traced here: 43.1 us
  blocking collectives  27.7 us (64%)
  Pallas kernels  9.37 us (22%)
  starting transfers between devices  5.24 us (12%)
  between operations  0.73 us (2%)
    all_to_all x1, blocking collectives, local(): lax.all_to_all(msg.reshape(peers, 4, LANES), 'tile', split_axis=0, concat...  16.7 us
    all_to_all x1, blocking collectives, local(): sums = lax.all_to_all(sums, 'tile', split_axis=0, concat_axis=0, tiled=True)  11 us
    pallas_call x1, Pallas kernels, local(): pl.pallas_call(route_kernel, out_shape=(array(OWN, width), array(OWN, wid...  7.01 us
    ppermute x1, starting transfers between devices, local(): near = lax.ppermute(near, 'tile', [(i, i ^ 1) for i in range(peers)])  3.33 us
    ppermute x1, starting transfers between devices, local(): lax.ppermute(far, 'tile', [(i, (i + 1 ^ 1) - 1) for i in range(1, peers -...  1.91 us
    pallas_call x1, Pallas kernels, local(): pl.pallas_call(send_kernel, out_shape=(array(4 * peers, LANES), array(40,...  1.4 us
    pallas_call x1, Pallas kernels, local(): pl.pallas_call(reach_kernel, out_shape=array(16, LANES), in_specs=[vmem]...  0.97 us
  transfers between devices with their start and end apart: 2, of which 0 were waited for; matrix products, arithmetic and copies ran while one was open for 0% of the time, Pallas kernels for 0%

profile of v6, /device:TPU:1, one launch (start us, length us, event | category | flops | bytes accessed | tf_op | source)
XLA Modules:
  0.0 43.1 jit_solution(7607075662737033377)
XLA Ops:
  0.6 0.0 copy-start
  0.6 0.0 copy-start.1
  0.7 0.0 copy-start.2
  0.7 0.0 copy-start.3
  0.7 0.0 copy-start.4
  0.7 1.4 %send.1 = (f32[128,128]{1,0:T(8,128)S(1)}, f32[40,2048]{1,0:T(8,128)S(1)}, f32[40,2048]{1,0:T(8,128)S(1)}) custom-call(f32[16,256]{1,0:T(8,128)} %precip.3, f32[16,256]{1,0:T(8,128)} %soil_init.3, f32[16,256]{1,0:T(8,128)} %ksat.3, s32[16,256]{1,0:T(8,128)} %land_mask.3, s32[16,128]{1,0:T(8,128)} %bitcast.13, f32[32,2048]{1,0:T(8,128)} %head_init.1, ...), custom_call_target="tpu_custom_call" | custom-call | tf_op jit(solution)/shard_map/send/pallas_call | solution.py:329
  2.1 3.3 %collective-permute-start = (f32[40,2048]{1,0:T(8,128)S(1)}, f32[40,2048]{1,0:T(8,128)S(1)}, u32[]{:S(2)}, u32[]{:S(2)}) collective-permute-start(f32[40,2048]{1,0:T(8,128)S(1)} %get-tuple-element.12), channel_id=1, source_target_pairs={{0,1},{1,0},{2,3},{3,2},{4,5},{5,4},{6,7},{7,6},{8,9},{9,8},{10,11... | collective-permute-start | bytes 983048 | tf_op jit(solution)/shard_map/ppermute | solution.py:355
  5.4 1.9 %collective-permute-start.1 = (f32[40,2048]{1,0:T(8,128)S(1)}, f32[40,2048]{1,0:T(8,128)S(1)}, u32[]{:S(2)}, u32[]{:S(2)}) collective-permute-start(f32[40,2048]{1,0:T(8,128)S(1)} %get-tuple-element.13), channel_id=1, source_target_pairs={{1,2},{2,1},{3,4},{4,3},{5,6},{6,5},{7,8},{8,7},{9,10},{10,9},{11,... | collective-permute-start | bytes 983048 | tf_op jit(solution)/shard_map/ppermute | solution.py:356
  7.3 16.7 %all_to_all.16 = f32[32,4,128]{2,1,0:T(4,128)S(1)} all-to-all(f32[32,4,128]{2,1,0:T(4,128)S(1)} %bitcast.10), channel_id=1, replica_groups=mesh['member'=8,'tile'=32] {'tile'}, dimensions={0} | all-to-all | bytes 131072 | tf_op jit(solution)/shard_map/all_to_all | solution.py:357
  24.0 0.0 collective-permute-done.near
  24.0 0.0 collective-permute-done.1.far
  24.0 0.0 copy-done
  24.0 0.0 copy-done.1
  24.0 0.0 copy-done.2
  24.1 0.0 copy-done.3
  24.1 0.0 copy-done.4
  24.1 7.0 %route.1 = (f32[32,2048]{1,0:T(8,128)}, f32[32,2048]{1,0:T(8,128)}, f32[32,128]{1,0:T(8,128)S(1)}, f32[16,256]{1,0:T(8,128)}) custom-call(f32[128,128]{1,0:T(8,128)S(1)} %bitcast.8, f32[32,2048]{1,0:T(8,128)S(1)} %copy-done, f32[32,2048]{1,0:T(8,128)S(1)} %copy-done.1, f32[32,2048]{1,0:T(8,128)S(1)} %copy-done.2, f32[32,2048]{1,0:T(8,128)S(1)} %copy-done.3, ...), custom_call_target="tpu_custom_call" | custom-call | tf_op jit(solution)/shard_map/route/pallas_call | solution.py:363
  31.1 11.0 %all_to_all.17 = f32[32,1,128]{2,1,0:T(1,128)S(1)} all-to-all(f32[32,1,128]{2,1,0:T(1,128)S(1)} %bitcast.12), channel_id=1, replica_groups=mesh['member'=8,'tile'=32] {'tile'}, dimensions={0} | all-to-all | bytes 32768 | tf_op jit(solution)/shard_map/all_to_all | solution.py:382
  42.1 1.0 %reach_sums.1 = f32[16,128]{1,0:T(8,128)} custom-call(f32[128,128]{1,0:T(8,128)S(1)} %bitcast.9, f32[32,128]{1,0:T(8,128)S(1)} %bitcast.11), custom_call_target="tpu_custom_call" | custom-call | tf_op jit(solution)/shard_map/reach_sums/pallas_call | solution.py:383
Async XLA Ops:
  0.6 23.4 %copy-start = (f32[32,2048]{1,0:T(8,128)S(1)}, f32[32,2048]{1,0:T(8,128)}, u32[]{:S(2)}) copy-start(f32[32,2048]{1,0:T(8,128)} %head_init.1) | copy-start | bytes 786436
  0.6 23.4 %copy-start.1 = (f32[32,2048]{1,0:T(8,128)S(1)}, f32[32,2048]{1,0:T(8,128)}, u32[]{:S(2)}) copy-start(f32[32,2048]{1,0:T(8,128)} %sub_init.1) | copy-start | bytes 786436
  0.7 23.4 %copy-start.2 = (f32[32,2048]{1,0:T(8,128)S(1)}, f32[32,2048]{1,0:T(8,128)}, u32[]{:S(2)}) copy-start(f32[32,2048]{1,0:T(8,128)} %conduct.3) | copy-start | bytes 786436
  0.7 23.4 %copy-start.3 = (f32[32,2048]{1,0:T(8,128)S(1)}, f32[32,2048]{1,0:T(8,128)}, u32[]{:S(2)}) copy-start(f32[32,2048]{1,0:T(8,128)} %drain.3) | copy-start | bytes 786436
  0.7 23.4 %copy-start.4 = (s32[32,2048]{1,0:T(8,128)S(1)}, s32[32,2048]{1,0:T(8,128)}, u32[]{:S(2)}) copy-start(s32[32,2048]{1,0:T(8,128)} %code.3) | copy-start | bytes 786436
  2.1 21.9 %collective-permute-start = (f32[40,2048]{1,0:T(8,128)S(1)}, f32[40,2048]{1,0:T(8,128)S(1)}, u32[]{:S(2)}, u32[]{:S(2)}) collective-permute-start(f32[40,2048]{1,0:T(8,128)S(1)} %get-tuple-element.12), channel_id=1, source_target_pairs={{0,1},{1,0},{2,3},{3,2},{4,5},{5,4},{6,7},{7,6},{8,9},{9,8},{10,11... | collective-permute-start | bytes 983048 | tf_op jit(solution)/shard_map/ppermute | solution.py:355
  5.4 18.6 %collective-permute-start.1 = (f32[40,2048]{1,0:T(8,128)S(1)}, f32[40,2048]{1,0:T(8,128)S(1)}, u32[]{:S(2)}, u32[]{:S(2)}) collective-permute-start(f32[40,2048]{1,0:T(8,128)S(1)} %get-tuple-element.13), channel_id=1, source_target_pairs={{1,2},{2,1},{3,4},{4,3},{5,6},{6,5},{7,8},{8,7},{9,10},{10,9},{11,... | collective-permute-start | bytes 983048 | tf_op jit(solution)/shard_map/ppermute | solution.py:356

commit v7 on v6

--- a/solution.py
+++ b/solution.py
@@ -104,7 +104,7 @@
     precip, pet, soil_init, ksat, land_mask,
     head_out, sub_out, msg, soil_out,
     turned, h_a, h_b, s_a, s_b, g_w, a_w, dn_w, up_w, rt_w, lf_w, kp_w,
-    head, sub, shares, slots, parts, fields_in, mask_in, soil, sem,
+    head, sub, shares, slots, parts, fields_in, mask_in, soil, shifted, sem,
 ):
     tiles = g_w.shape[0]
     width = tiles * LANES
@@ -184,6 +184,10 @@
                 h_a[j, here, :] = h0[:, cut(u)]
                 s_a[j, here, :] = s0[:, cut(u)]
 
+    edge = jnp.zeros((3, tiles, 8, LANES), F32)
+    shifted[:, :, 0:8, :] = edge
+    shifted[:, :, ROWS + 8 : ROWS + 16, :] = edge
+
     def products(j, h_in, s_in):
         p = g_w[j] * h_in[j]
         s = s_in[j]
@@ -202,14 +206,19 @@
             after = products(j + 1, h_in, s_in) if j < tiles - 1 else (zero,) * 5
             p = now[0]
             s = s_in[j]
-            flux = pltpu.roll(p, 1, 0) + pltpu.roll(p, ROWS - 1, 0)
-            flux = flux + left_of(now[1], before[1])
-            flux = flux + right_of(now[2], after[2])
-            new = pltpu.roll(dn_w[j] * s, 1, 0) + pltpu.roll(up_w[j] * s, ROWS - 1, 0)
-            new = new + left_of(now[3], before[3])
-            new = new + right_of(now[4], after[4])
-            h = a_w[j, keep, :] * h_in[j, keep, :] + g_w[j, keep, :] * flux[keep]
-            take(j, h, new[keep] + kp_w[j, keep, :] * s[keep])
+            shifted[0, j, 8 : ROWS + 8, :] = p
+            above_at = slice(keep.start + 7, keep.stop + 7)
+            below_at = slice(keep.start + 9, keep.stop + 9)
+            flux = shifted[0, j, above_at, :] + shifted[0, j, below_at, :]
+            flux = flux + left_of(now[1], before[1])[keep]
+            flux = flux + right_of(now[2], after[2])[keep]
+            shifted[1, j, 8 : ROWS + 8, :] = dn_w[j] * s
+            shifted[2, j, 8 : ROWS + 8, :] = up_w[j] * s
+            new = shifted[1, j, above_at, :] + shifted[2, j, below_at, :]
+            new = new + left_of(now[3], before[3])[keep]
+            new = new + right_of(now[4], after[4])[keep]
+            h = a_w[j, keep, :] * h_in[j, keep, :] + g_w[j, keep, :] * flux
+            take(j, h, new + kp_w[j, keep, :] * s[keep])
             before, now = now, after
 
     def store(h_to, s_to):
@@ -372,7 +381,8 @@
         + [plane] * 3
         + [pltpu.VMEM((OWN, width), jnp.int32), pltpu.VMEM((4, OWN, width), F32)]
         + [pltpu.VMEM((4,) + precip.shape, F32), pltpu.VMEM(precip.shape, jnp.int32)]
-        + [pltpu.VMEM(precip.shape, F32), pltpu.SemaphoreType.DMA((10,))],
+        + [pltpu.VMEM(precip.shape, F32), pltpu.VMEM((3, tiles, ROWS + 16, LANES), F32)]
+        + [pltpu.SemaphoreType.DMA((10,))],
         compiler_params=pltpu.CompilerParams(vmem_limit_bytes=16 * MIB),
         name="route",
     )(

time: 43.3 us -> 43.1 us (level)
  no operation moved by 1% of the time
where the time goes in v7:
time: 43.1 us; the launch traced here: 42.9 us
  blocking collectives  27.7 us (64%)
  Pallas kernels  9.17 us (21%)
  starting transfers between devices  5.24 us (12%)
  between operations  0.73 us (2%)
    all_to_all x1, blocking collectives, local(): lax.all_to_all(msg.reshape(peers, 4, LANES), 'tile', split_axis=0, concat...  16.7 us
    all_to_all x1, blocking collectives, local(): sums = lax.all_to_all(sums, 'tile', split_axis=0, concat_axis=0, tiled=True)  11 us
    pallas_call x1, Pallas kernels, local(): pl.pallas_call(route_kernel, out_shape=(array(OWN, width), array(OWN, wid...  6.81 us
    ppermute x1, starting transfers between devices, local(): near = lax.ppermute(near, 'tile', [(i, i ^ 1) for i in range(peers)])  3.33 us
    ppermute x1, starting transfers between devices, local(): lax.ppermute(far, 'tile', [(i, (i + 1 ^ 1) - 1) for i in range(1, peers -...  1.91 us
    pallas_call x1, Pallas kernels, local(): pl.pallas_call(send_kernel, out_shape=(array(4 * peers, LANES), array(40,...  1.4 us
    pallas_call x1, Pallas kernels, local(): pl.pallas_call(reach_kernel, out_shape=array(16, LANES), in_specs=[vmem]...  0.96 us
  transfers between devices with their start and end apart: 2, of which 0 were waited for; matrix products, arithmetic and copies ran while one was open for 0% of the time, Pallas kernels for 0%

profile of v7, /device:TPU:1, one launch (start us, length us, event | category | flops | bytes accessed | tf_op | source)
XLA Modules:
  0.0 42.9 jit_solution(8723349093704010360)
XLA Ops:
  0.6 0.0 copy-start
  0.6 0.0 copy-start.1
  0.7 0.0 copy-start.2
  0.7 0.0 copy-start.3
  0.7 0.0 copy-start.4
  0.7 1.4 %send.1 = (f32[128,128]{1,0:T(8,128)S(1)}, f32[40,2048]{1,0:T(8,128)S(1)}, f32[40,2048]{1,0:T(8,128)S(1)}) custom-call(f32[16,256]{1,0:T(8,128)} %precip.3, f32[16,256]{1,0:T(8,128)} %soil_init.3, f32[16,256]{1,0:T(8,128)} %ksat.3, s32[16,256]{1,0:T(8,128)} %land_mask.3, s32[16,128]{1,0:T(8,128)} %bitcast.13, f32[32,2048]{1,0:T(8,128)} %head_init.1, ...), custom_call_target="tpu_custom_call" | custom-call | tf_op jit(solution)/shard_map/send/pallas_call | solution.py:338
  2.1 3.3 %collective-permute-start = (f32[40,2048]{1,0:T(8,128)S(1)}, f32[40,2048]{1,0:T(8,128)S(1)}, u32[]{:S(2)}, u32[]{:S(2)}) collective-permute-start(f32[40,2048]{1,0:T(8,128)S(1)} %get-tuple-element.12), channel_id=1, source_target_pairs={{0,1},{1,0},{2,3},{3,2},{4,5},{5,4},{6,7},{7,6},{8,9},{9,8},{10,11... | collective-permute-start | bytes 983048 | tf_op jit(solution)/shard_map/ppermute | solution.py:364
  5.4 1.9 %collective-permute-start.1 = (f32[40,2048]{1,0:T(8,128)S(1)}, f32[40,2048]{1,0:T(8,128)S(1)}, u32[]{:S(2)}, u32[]{:S(2)}) collective-permute-start(f32[40,2048]{1,0:T(8,128)S(1)} %get-tuple-element.13), channel_id=1, source_target_pairs={{1,2},{2,1},{3,4},{4,3},{5,6},{6,5},{7,8},{8,7},{9,10},{10,9},{11,... | collective-permute-start | bytes 983048 | tf_op jit(solution)/shard_map/ppermute | solution.py:365
  7.3 16.7 %all_to_all.16 = f32[32,4,128]{2,1,0:T(4,128)S(1)} all-to-all(f32[32,4,128]{2,1,0:T(4,128)S(1)} %bitcast.10), channel_id=1, replica_groups=mesh['member'=8,'tile'=32] {'tile'}, dimensions={0} | all-to-all | bytes 131072 | tf_op jit(solution)/shard_map/all_to_all | solution.py:366
  24.0 0.0 collective-permute-done.near
  24.0 0.0 collective-permute-done.1.far
  24.0 0.0 copy-done
  24.0 0.0 copy-done.1
  24.0 0.0 copy-done.2
  24.1 0.0 copy-done.3
  24.1 0.0 copy-done.4
  24.1 6.8 %route.1 = (f32[32,2048]{1,0:T(8,128)}, f32[32,2048]{1,0:T(8,128)}, f32[32,128]{1,0:T(8,128)S(1)}, f32[16,256]{1,0:T(8,128)}) custom-call(f32[128,128]{1,0:T(8,128)S(1)} %bitcast.8, f32[32,2048]{1,0:T(8,128)S(1)} %copy-done, f32[32,2048]{1,0:T(8,128)S(1)} %copy-done.1, f32[32,2048]{1,0:T(8,128)S(1)} %copy-done.2, f32[32,2048]{1,0:T(8,128)S(1)} %copy-done.3, ...), custom_call_target="tpu_custom_call" | custom-call | tf_op jit(solution)/shard_map/route/pallas_call | solution.py:372
  30.9 11.0 %all_to_all.17 = f32[32,1,128]{2,1,0:T(1,128)S(1)} all-to-all(f32[32,1,128]{2,1,0:T(1,128)S(1)} %bitcast.12), channel_id=1, replica_groups=mesh['member'=8,'tile'=32] {'tile'}, dimensions={0} | all-to-all | bytes 32768 | tf_op jit(solution)/shard_map/all_to_all | solution.py:392
  41.9 1.0 %reach_sums.1 = f32[16,128]{1,0:T(8,128)} custom-call(f32[128,128]{1,0:T(8,128)S(1)} %bitcast.9, f32[32,128]{1,0:T(8,128)S(1)} %bitcast.11), custom_call_target="tpu_custom_call" | custom-call | tf_op jit(solution)/shard_map/reach_sums/pallas_call | solution.py:393
Async XLA Ops:
  0.6 23.4 %copy-start = (f32[32,2048]{1,0:T(8,128)S(1)}, f32[32,2048]{1,0:T(8,128)}, u32[]{:S(2)}) copy-start(f32[32,2048]{1,0:T(8,128)} %head_init.1) | copy-start | bytes 786436
  0.6 23.4 %copy-start.1 = (f32[32,2048]{1,0:T(8,128)S(1)}, f32[32,2048]{1,0:T(8,128)}, u32[]{:S(2)}) copy-start(f32[32,2048]{1,0:T(8,128)} %sub_init.1) | copy-start | bytes 786436
  0.7 23.4 %copy-start.2 = (f32[32,2048]{1,0:T(8,128)S(1)}, f32[32,2048]{1,0:T(8,128)}, u32[]{:S(2)}) copy-start(f32[32,2048]{1,0:T(8,128)} %conduct.3) | copy-start | bytes 786436
  0.7 23.4 %copy-start.3 = (f32[32,2048]{1,0:T(8,128)S(1)}, f32[32,2048]{1,0:T(8,128)}, u32[]{:S(2)}) copy-start(f32[32,2048]{1,0:T(8,128)} %drain.3) | copy-start | bytes 786436
  0.7 23.4 %copy-start.4 = (s32[32,2048]{1,0:T(8,128)S(1)}, s32[32,2048]{1,0:T(8,128)}, u32[]{:S(2)}) copy-start(s32[32,2048]{1,0:T(8,128)} %code.3) | copy-start | bytes 786436
  2.1 21.9 %collective-permute-start = (f32[40,2048]{1,0:T(8,128)S(1)}, f32[40,2048]{1,0:T(8,128)S(1)}, u32[]{:S(2)}, u32[]{:S(2)}) collective-permute-start(f32[40,2048]{1,0:T(8,128)S(1)} %get-tuple-element.12), channel_id=1, source_target_pairs={{0,1},{1,0},{2,3},{3,2},{4,5},{5,4},{6,7},{7,6},{8,9},{9,8},{10,11... | collective-permute-start | bytes 983048 | tf_op jit(solution)/shard_map/ppermute | solution.py:364
  5.4 18.6 %collective-permute-start.1 = (f32[40,2048]{1,0:T(8,128)S(1)}, f32[40,2048]{1,0:T(8,128)S(1)}, u32[]{:S(2)}, u32[]{:S(2)}) collective-permute-start(f32[40,2048]{1,0:T(8,128)S(1)} %get-tuple-element.13), channel_id=1, source_target_pairs={{1,2},{2,1},{3,4},{4,3},{5,6},{6,5},{7,8},{8,7},{9,10},{10,9},{11,... | collective-permute-start | bytes 983048 | tf_op jit(solution)/shard_map/ppermute | solution.py:365

commit v8 on v7

--- a/solution.py
+++ b/solution.py
@@ -188,63 +188,74 @@
     shifted[:, :, 0:8, :] = edge
     shifted[:, :, ROWS + 8 : ROWS + 16, :] = edge
 
-    def products(j, h_in, s_in):
-        p = g_w[j] * h_in[j]
-        s = s_in[j]
-        return (
-            p,
-            pltpu.roll(p, 1, 1),
-            pltpu.roll(p, LANES - 1, 1),
-            pltpu.roll(rt_w[j] * s, 1, 1),
-            pltpu.roll(lf_w[j] * s, LANES - 1, 1),
-        )
-
-    def substep(h_in, s_in, keep, take):
-        before = (zero,) * 5
-        now = products(0, h_in, s_in)
+    def around(keep):
+        up_rows = slice(keep.start + 7, keep.stop + 7)
+        down_rows = slice(keep.start + 9, keep.stop + 9)
+        return up_rows, down_rows
+
+    def head_step(h_in, keep, take):
+        above_at, below_at = around(keep)
+
+        def products(j):
+            p = g_w[j] * h_in[j]
+            return p, pltpu.roll(p, 1, 1), pltpu.roll(p, LANES - 1, 1)
+
+        before = zero
+        now = products(0)
         for j in range(tiles):
-            after = products(j + 1, h_in, s_in) if j < tiles - 1 else (zero,) * 5
-            p = now[0]
+            after = products(j + 1) if j < tiles - 1 else (zero,) * 3
+            shifted[0, j, 8 : ROWS + 8, :] = now[0]
+            flux = shifted[0, j, above_at, :] + shifted[0, j, below_at, :]
+            flux = flux + left_of(now[1], before)[keep]
+            flux = flux + right_of(now[2], after[2])[keep]
+            take(j, a_w[j, keep, :] * h_in[j, keep, :] + g_w[j, keep, :] * flux)
+            before, now = now[1], after
+
+    def sub_step(s_in, keep, take):
+        above_at, below_at = around(keep)
+
+        def products(j):
             s = s_in[j]
-            shifted[0, j, 8 : ROWS + 8, :] = p
-            above_at = slice(keep.start + 7, keep.stop + 7)
-            below_at = slice(keep.start + 9, keep.stop + 9)
-            flux = shifted[0, j, above_at, :] + shifted[0, j, below_at, :]
-            flux = flux + left_of(now[1], before[1])[keep]
-            flux = flux + right_of(now[2], after[2])[keep]
+            return pltpu.roll(rt_w[j] * s, 1, 1), pltpu.roll(lf_w[j] * s, LANES - 1, 1)
+
+        before = zero
+        now = products(0)
+        for j in range(tiles):
+            after = products(j + 1) if j < tiles - 1 else (zero,) * 2
+            s = s_in[j]
             shifted[1, j, 8 : ROWS + 8, :] = dn_w[j] * s
             shifted[2, j, 8 : ROWS + 8, :] = up_w[j] * s
             new = shifted[1, j, above_at, :] + shifted[2, j, below_at, :]
-            new = new + left_of(now[3], before[3])[keep]
-            new = new + right_of(now[4], after[4])[keep]
-            h = a_w[j, keep, :] * h_in[j, keep, :] + g_w[j, keep, :] * flux
-            take(j, h, new + kp_w[j, keep, :] * s[keep])
-            before, now = now, after
-
-    def store(h_to, s_to):
-        def take(j, h, s):
-            h_to[j] = h
-            s_to[j] = s
+            new = new + left_of(now[0], before)[keep]
+            new = new + right_of(now[1], after[1])[keep]
+            take(j, new + kp_w[j, keep, :] * s[keep])
+            before, now = now[0], after
+
+    def store(to):
+        def take(j, x):
+            to[j] = x
 
         return take
 
-    def finish(j, h, s):
+    def finish_sub(j, s):
+        sub[:, cut(j)] = s
+
+    def finish(j, h):
         at = cut(j)
-        sub[:, at] = s
         inflow = shares[:, at] * h
         head[:, at] = h - inflow
         coarse = inflow.astype(BF16).astype(F32)
         parts[0, :, at] = coarse
         parts[1, :, at] = inflow - coarse
-        q = slots[:, at]
-        parts[2, :, at] = (q >> 6).astype(F32)
-        parts[3, :, at] = (q & 63).astype(F32)
 
     source = (h_a, s_a)
     target = (h_b, s_b)
     for i in range(ITERS - 1):
-        substep(*source, slice(0, ROWS), store(*target))
+        sub_step(source[1], slice(0, ROWS), store(target[1]))
         source, target = target, source
+    sub_step(source[1], slice(HALO, HALO + OWN), finish_sub)
+    sub_copy = pltpu.make_async_copy(sub, sub_out, sem.at[2])
+    sub_copy.start()
     for c in local:
         c.wait()
     mask = mask_in[...].astype(F32)
@@ -256,11 +267,15 @@
     soil_copy.start()
     share_copy.wait()
     slot_copy.wait()
-    substep(*source, slice(HALO, HALO + OWN), finish)
+    parts[2] = (slots[...] >> 6).astype(F32)
+    parts[3] = (slots[...] & 63).astype(F32)
+    source, target = (h_a, s_a), (h_b, s_b)
+    for i in range(ITERS - 1):
+        head_step(source[0], slice(0, ROWS), store(target[0]))
+        source, target = target, source
+    head_step(source[0], slice(HALO, HALO + OWN), finish)
     head_copy = pltpu.make_async_copy(head, head_out, sem.at[1])
-    sub_copy = pltpu.make_async_copy(sub, sub_out, sem.at[2])
     head_copy.start()
-    sub_copy.start()
 
     owner = iota((32, width), 0).astype(F32).astype(BF16)
     place = iota((64, width), 0).astype(F32).astype(BF16)

time: 43.1 us -> 42.8 us (level)
  no operation moved by 1% of the time
where the time goes in v8:
time: 42.8 us; the launch traced here: 42.5 us
  blocking collectives  27.7 us (65%)
  Pallas kernels  8.85 us (21%)
  starting transfers between devices  5.24 us (12%)
  between operations  0.73 us (2%)
    all_to_all x1, blocking collectives, local(): lax.all_to_all(msg.reshape(peers, 4, LANES), 'tile', split_axis=0, concat...  16.7 us
    all_to_all x1, blocking collectives, local(): sums = lax.all_to_all(sums, 'tile', split_axis=0, concat_axis=0, tiled=True)  11 us
    pallas_call x1, Pallas kernels, local(): pl.pallas_call(route_kernel, out_shape=(array(OWN, width), array(OWN, wid...  6.49 us
    ppermute x1, starting transfers between devices, local(): near = lax.ppermute(near, 'tile', [(i, i ^ 1) for i in range(peers)])  3.33 us
    ppermute x1, starting transfers between devices, local(): lax.ppermute(far, 'tile', [(i, (i + 1 ^ 1) - 1) for i in range(1, peers -...  1.91 us
    pallas_call x1, Pallas kernels, local(): pl.pallas_call(send_kernel, out_shape=(array(4 * peers, LANES), array(40,...  1.4 us
    pallas_call x1, Pallas kernels, local(): pl.pallas_call(reach_kernel, out_shape=array(16, LANES), in_specs=[vmem]...  0.96 us
  transfers between devices with their start and end apart: 2, of which 0 were waited for; matrix products, arithmetic and copies ran while one was open for 0% of the time, Pallas kernels for 0%

profile of v8, /device:TPU:1, one launch (start us, length us, event | category | flops | bytes accessed | tf_op | source)
XLA Modules:
  0.0 42.5 jit_solution(9069971586559935590)
XLA Ops:
  0.6 0.0 copy-start
  0.6 0.0 copy-start.1
  0.7 0.0 copy-start.2
  0.7 0.0 copy-start.3
  0.7 0.0 copy-start.4
  0.7 1.4 %send.1 = (f32[128,128]{1,0:T(8,128)S(1)}, f32[40,2048]{1,0:T(8,128)S(1)}, f32[40,2048]{1,0:T(8,128)S(1)}) custom-call(f32[16,256]{1,0:T(8,128)} %precip.3, f32[16,256]{1,0:T(8,128)} %soil_init.3, f32[16,256]{1,0:T(8,128)} %ksat.3, s32[16,256]{1,0:T(8,128)} %land_mask.3, s32[16,128]{1,0:T(8,128)} %bitcast.13, f32[32,2048]{1,0:T(8,128)} %head_init.1, ...), custom_call_target="tpu_custom_call" | custom-call | tf_op jit(solution)/shard_map/send/pallas_call | solution.py:353
  2.1 3.3 %collective-permute-start = (f32[40,2048]{1,0:T(8,128)S(1)}, f32[40,2048]{1,0:T(8,128)S(1)}, u32[]{:S(2)}, u32[]{:S(2)}) collective-permute-start(f32[40,2048]{1,0:T(8,128)S(1)} %get-tuple-element.12), channel_id=1, source_target_pairs={{0,1},{1,0},{2,3},{3,2},{4,5},{5,4},{6,7},{7,6},{8,9},{9,8},{10,11... | collective-permute-start | bytes 983048 | tf_op jit(solution)/shard_map/ppermute | solution.py:379
  5.4 1.9 %collective-permute-start.1 = (f32[40,2048]{1,0:T(8,128)S(1)}, f32[40,2048]{1,0:T(8,128)S(1)}, u32[]{:S(2)}, u32[]{:S(2)}) collective-permute-start(f32[40,2048]{1,0:T(8,128)S(1)} %get-tuple-element.13), channel_id=1, source_target_pairs={{1,2},{2,1},{3,4},{4,3},{5,6},{6,5},{7,8},{8,7},{9,10},{10,9},{11,... | collective-permute-start | bytes 983048 | tf_op jit(solution)/shard_map/ppermute | solution.py:380
  7.3 16.7 %all_to_all.16 = f32[32,4,128]{2,1,0:T(4,128)S(1)} all-to-all(f32[32,4,128]{2,1,0:T(4,128)S(1)} %bitcast.10), channel_id=1, replica_groups=mesh['member'=8,'tile'=32] {'tile'}, dimensions={0} | all-to-all | bytes 131072 | tf_op jit(solution)/shard_map/all_to_all | solution.py:381
  24.0 0.0 collective-permute-done.near
  24.0 0.0 collective-permute-done.1.far
  24.0 0.0 copy-done
  24.0 0.0 copy-done.1
  24.0 0.0 copy-done.2
  24.1 0.0 copy-done.3
  24.1 0.0 copy-done.4
  24.1 6.5 %route.1 = (f32[32,2048]{1,0:T(8,128)}, f32[32,2048]{1,0:T(8,128)}, f32[32,128]{1,0:T(8,128)S(1)}, f32[16,256]{1,0:T(8,128)}) custom-call(f32[128,128]{1,0:T(8,128)S(1)} %bitcast.8, f32[32,2048]{1,0:T(8,128)S(1)} %copy-done, f32[32,2048]{1,0:T(8,128)S(1)} %copy-done.1, f32[32,2048]{1,0:T(8,128)S(1)} %copy-done.2, f32[32,2048]{1,0:T(8,128)S(1)} %copy-done.3, ...), custom_call_target="tpu_custom_call" | custom-call | tf_op jit(solution)/shard_map/route/pallas_call | solution.py:387
  30.6 11.0 %all_to_all.17 = f32[32,1,128]{2,1,0:T(1,128)S(1)} all-to-all(f32[32,1,128]{2,1,0:T(1,128)S(1)} %bitcast.12), channel_id=1, replica_groups=mesh['member'=8,'tile'=32] {'tile'}, dimensions={0} | all-to-all | bytes 32768 | tf_op jit(solution)/shard_map/all_to_all | solution.py:407
  41.6 1.0 %reach_sums.1 = f32[16,128]{1,0:T(8,128)} custom-call(f32[128,128]{1,0:T(8,128)S(1)} %bitcast.9, f32[32,128]{1,0:T(8,128)S(1)} %bitcast.11), custom_call_target="tpu_custom_call" | custom-call | tf_op jit(solution)/shard_map/reach_sums/pallas_call | solution.py:408
Async XLA Ops:
  0.6 23.4 %copy-start = (f32[32,2048]{1,0:T(8,128)S(1)}, f32[32,2048]{1,0:T(8,128)}, u32[]{:S(2)}) copy-start(f32[32,2048]{1,0:T(8,128)} %head_init.1) | copy-start | bytes 786436
  0.6 23.4 %copy-start.1 = (f32[32,2048]{1,0:T(8,128)S(1)}, f32[32,2048]{1,0:T(8,128)}, u32[]{:S(2)}) copy-start(f32[32,2048]{1,0:T(8,128)} %sub_init.1) | copy-start | bytes 786436
  0.7 23.4 %copy-start.2 = (f32[32,2048]{1,0:T(8,128)S(1)}, f32[32,2048]{1,0:T(8,128)}, u32[]{:S(2)}) copy-start(f32[32,2048]{1,0:T(8,128)} %conduct.3) | copy-start | bytes 786436
  0.7 23.4 %copy-start.3 = (f32[32,2048]{1,0:T(8,128)S(1)}, f32[32,2048]{1,0:T(8,128)}, u32[]{:S(2)}) copy-start(f32[32,2048]{1,0:T(8,128)} %drain.3) | copy-start | bytes 786436
  0.7 23.4 %copy-start.4 = (s32[32,2048]{1,0:T(8,128)S(1)}, s32[32,2048]{1,0:T(8,128)}, u32[]{:S(2)}) copy-start(s32[32,2048]{1,0:T(8,128)} %code.3) | copy-start | bytes 786436
  2.1 21.9 %collective-permute-start = (f32[40,2048]{1,0:T(8,128)S(1)}, f32[40,2048]{1,0:T(8,128)S(1)}, u32[]{:S(2)}, u32[]{:S(2)}) collective-permute-start(f32[40,2048]{1,0:T(8,128)S(1)} %get-tuple-element.12), channel_id=1, source_target_pairs={{0,1},{1,0},{2,3},{3,2},{4,5},{5,4},{6,7},{7,6},{8,9},{9,8},{10,11... | collective-permute-start | bytes 983048 | tf_op jit(solution)/shard_map/ppermute | solution.py:379
  5.4 18.6 %collective-permute-start.1 = (f32[40,2048]{1,0:T(8,128)S(1)}, f32[40,2048]{1,0:T(8,128)S(1)}, u32[]{:S(2)}, u32[]{:S(2)}) collective-permute-start(f32[40,2048]{1,0:T(8,128)S(1)} %get-tuple-element.13), channel_id=1, source_target_pairs={{1,2},{2,1},{3,4},{4,3},{5,6},{6,5},{7,8},{8,7},{9,10},{10,9},{11,... | collective-permute-start | bytes 983048 | tf_op jit(solution)/shard_map/ppermute | solution.py:380

commit v9 on v8

--- a/solution.py
+++ b/solution.py
@@ -140,7 +140,10 @@
         d = window(drain, 3, j)
         k = window(code, 4, j)
         moves = [jnp.where(k == float(i), d, 0.0) for i in range(4)]
-        dn_w[j], up_w[j], rt_w[j], lf_w[j] = moves
+        dn_w[j] = pltpu.roll(moves[0], 1, 0)
+        up_w[j] = pltpu.roll(moves[1], ROWS - 1, 0)
+        rt_w[j] = moves[2]
+        lf_w[j] = moves[3]
         kp_w[j] = 1.0 - (moves[0] + moves[1] + moves[2] + moves[3])
     for j in range(tiles):
         g = g_w[j]
@@ -182,11 +185,13 @@
             for u in range(2):
                 j = 2 * n + u
                 h_a[j, here, :] = h0[:, cut(u)]
-                s_a[j, here, :] = s0[:, cut(u)]
-
-    edge = jnp.zeros((3, tiles, 8, LANES), F32)
-    shifted[:, :, 0:8, :] = edge
-    shifted[:, :, ROWS + 8 : ROWS + 16, :] = edge
+                s_a[j, 8 * i + 8 : 8 * i + 16, :] = s0[:, cut(u)]
+
+    edge = jnp.zeros((tiles, 8, LANES), F32)
+    for ref in (shifted, s_a, s_b):
+        ref[:, 0:8, :] = edge
+        ref[:, ROWS + 8 : ROWS + 16, :] = edge
+    middle = slice(8, ROWS + 8)
 
     def around(keep):
         up_rows = slice(keep.start + 7, keep.stop + 7)
@@ -204,8 +209,8 @@
         now = products(0)
         for j in range(tiles):
             after = products(j + 1) if j < tiles - 1 else (zero,) * 3
-            shifted[0, j, 8 : ROWS + 8, :] = now[0]
-            flux = shifted[0, j, above_at, :] + shifted[0, j, below_at, :]
+            shifted[j, middle, :] = now[0]
+            flux = shifted[j, above_at, :] + shifted[j, below_at, :]
             flux = flux + left_of(now[1], before)[keep]
             flux = flux + right_of(now[2], after[2])[keep]
             take(j, a_w[j, keep, :] * h_in[j, keep, :] + g_w[j, keep, :] * flux)
@@ -215,25 +220,23 @@
         above_at, below_at = around(keep)
 
         def products(j):
-            s = s_in[j]
+            s = s_in[j, middle, :]
             return pltpu.roll(rt_w[j] * s, 1, 1), pltpu.roll(lf_w[j] * s, LANES - 1, 1)
 
         before = zero
         now = products(0)
         for j in range(tiles):
             after = products(j + 1) if j < tiles - 1 else (zero,) * 2
-            s = s_in[j]
-            shifted[1, j, 8 : ROWS + 8, :] = dn_w[j] * s
-            shifted[2, j, 8 : ROWS + 8, :] = up_w[j] * s
-            new = shifted[1, j, above_at, :] + shifted[2, j, below_at, :]
+            s = s_in[j, middle, :]
+            new = dn_w[j, keep, :] * s_in[j, above_at, :] + up_w[j, keep, :] * s_in[j, below_at, :]
             new = new + left_of(now[0], before)[keep]
             new = new + right_of(now[1], after[1])[keep]
             take(j, new + kp_w[j, keep, :] * s[keep])
             before, now = now[0], after
 
-    def store(to):
+    def store(to, rows):
         def take(j, x):
-            to[j] = x
+            to[j, rows, :] = x
 
         return take
 
@@ -251,7 +254,7 @@
     source = (h_a, s_a)
     target = (h_b, s_b)
     for i in range(ITERS - 1):
-        sub_step(source[1], slice(0, ROWS), store(target[1]))
+        sub_step(source[1], slice(0, ROWS), store(target[1], middle))
         source, target = target, source
     sub_step(source[1], slice(HALO, HALO + OWN), finish_sub)
     sub_copy = pltpu.make_async_copy(sub, sub_out, sem.at[2])
@@ -271,7 +274,7 @@
     parts[3] = (slots[...] & 63).astype(F32)
     source, target = (h_a, s_a), (h_b, s_b)
     for i in range(ITERS - 1):
-        head_step(source[0], slice(0, ROWS), store(target[0]))
+        head_step(source[0], slice(0, ROWS), store(target[0], slice(0, ROWS)))
         source, target = target, source
     head_step(source[0], slice(HALO, HALO + OWN), finish)
     head_copy = pltpu.make_async_copy(head, head_out, sem.at[1])
@@ -392,11 +395,13 @@
         in_specs=[vmem] * 8 + [outside] * 7,
         out_specs=(outside, outside, vmem, outside),
         scratch_shapes=[pltpu.VMEM((384, LANES), F32)]
-        + [window] * 11
+        + [window] * 2
+        + [pltpu.VMEM((tiles, ROWS + 16, LANES), F32)] * 2
+        + [window] * 7
         + [plane] * 3
         + [pltpu.VMEM((OWN, width), jnp.int32), pltpu.VMEM((4, OWN, width), F32)]
         + [pltpu.VMEM((4,) + precip.shape, F32), pltpu.VMEM(precip.shape, jnp.int32)]
-        + [pltpu.VMEM(precip.shape, F32), pltpu.VMEM((3, tiles, ROWS + 16, LANES), F32)]
+        + [pltpu.VMEM(precip.shape, F32), pltpu.VMEM((tiles, ROWS + 16, LANES), F32)]
         + [pltpu.SemaphoreType.DMA((10,))],
         compiler_params=pltpu.CompilerParams(vmem_limit_bytes=16 * MIB),
         name="route",

time: 42.8 us -> 42.9 us (level)
  no operation moved by 1% of the time
where the time goes in v9:
time: 42.9 us; the launch traced here: 42.6 us
  blocking collectives  27.7 us (65%)
  Pallas kernels  8.91 us (21%)
  starting transfers between devices  5.24 us (12%)
  between operations  0.73 us (2%)
    all_to_all x1, blocking collectives, local(): lax.all_to_all(msg.reshape(peers, 4, LANES), 'tile', split_axis=0, concat...  16.7 us
    all_to_all x1, blocking collectives, local(): sums = lax.all_to_all(sums, 'tile', split_axis=0, concat_axis=0, tiled=True)  11 us
    pallas_call x1, Pallas kernels, local(): pl.pallas_call(route_kernel, out_shape=(array(OWN, width), array(OWN, wid...  6.55 us
    ppermute x1, starting transfers between devices, local(): near = lax.ppermute(near, 'tile', [(i, i ^ 1) for i in range(peers)])  3.33 us
    ppermute x1, starting transfers between devices, local(): lax.ppermute(far, 'tile', [(i, (i + 1 ^ 1) - 1) for i in range(1, peers -...  1.91 us
    pallas_call x1, Pallas kernels, local(): pl.pallas_call(send_kernel, out_shape=(array(4 * peers, LANES), array(40,...  1.4 us
    pallas_call x1, Pallas kernels, local(): pl.pallas_call(reach_kernel, out_shape=array(16, LANES), in_specs=[vmem]...  0.96 us
  transfers between devices with their start and end apart: 2, of which 0 were waited for; matrix products, arithmetic and copies ran while one was open for 0% of the time, Pallas kernels for 0%

profile of v9, /device:TPU:1, one launch (start us, length us, event | category | flops | bytes accessed | tf_op | source)
XLA Modules:
  0.0 42.6 jit_solution(11921628341409673394)
XLA Ops:
  0.6 0.0 copy-start
  0.6 0.0 copy-start.1
  0.7 0.0 copy-start.2
  0.7 0.0 copy-start.3
  0.7 0.0 copy-start.4
  0.7 1.4 %send.1 = (f32[128,128]{1,0:T(8,128)S(1)}, f32[40,2048]{1,0:T(8,128)S(1)}, f32[40,2048]{1,0:T(8,128)S(1)}) custom-call(f32[16,256]{1,0:T(8,128)} %precip.3, f32[16,256]{1,0:T(8,128)} %soil_init.3, f32[16,256]{1,0:T(8,128)} %ksat.3, s32[16,256]{1,0:T(8,128)} %land_mask.3, s32[16,128]{1,0:T(8,128)} %bitcast.13, f32[32,2048]{1,0:T(8,128)} %head_init.1, ...), custom_call_target="tpu_custom_call" | custom-call | tf_op jit(solution)/shard_map/send/pallas_call | solution.py:356
  2.1 3.3 %collective-permute-start = (f32[40,2048]{1,0:T(8,128)S(1)}, f32[40,2048]{1,0:T(8,128)S(1)}, u32[]{:S(2)}, u32[]{:S(2)}) collective-permute-start(f32[40,2048]{1,0:T(8,128)S(1)} %get-tuple-element.12), channel_id=1, source_target_pairs={{0,1},{1,0},{2,3},{3,2},{4,5},{5,4},{6,7},{7,6},{8,9},{9,8},{10,11... | collective-permute-start | bytes 983048 | tf_op jit(solution)/shard_map/ppermute | solution.py:382
  5.4 1.9 %collective-permute-start.1 = (f32[40,2048]{1,0:T(8,128)S(1)}, f32[40,2048]{1,0:T(8,128)S(1)}, u32[]{:S(2)}, u32[]{:S(2)}) collective-permute-start(f32[40,2048]{1,0:T(8,128)S(1)} %get-tuple-element.13), channel_id=1, source_target_pairs={{1,2},{2,1},{3,4},{4,3},{5,6},{6,5},{7,8},{8,7},{9,10},{10,9},{11,... | collective-permute-start | bytes 983048 | tf_op jit(solution)/shard_map/ppermute | solution.py:383
  7.3 16.7 %all_to_all.16 = f32[32,4,128]{2,1,0:T(4,128)S(1)} all-to-all(f32[32,4,128]{2,1,0:T(4,128)S(1)} %bitcast.10), channel_id=1, replica_groups=mesh['member'=8,'tile'=32] {'tile'}, dimensions={0} | all-to-all | bytes 131072 | tf_op jit(solution)/shard_map/all_to_all | solution.py:384
  24.0 0.0 collective-permute-done.near
  24.0 0.0 collective-permute-done.1.far
  24.0 0.0 copy-done
  24.0 0.0 copy-done.1
  24.0 0.0 copy-done.2
  24.1 0.0 copy-done.3
  24.1 0.0 copy-done.4
  24.1 6.6 %route.1 = (f32[32,2048]{1,0:T(8,128)}, f32[32,2048]{1,0:T(8,128)}, f32[32,128]{1,0:T(8,128)S(1)}, f32[16,256]{1,0:T(8,128)}) custom-call(f32[128,128]{1,0:T(8,128)S(1)} %bitcast.8, f32[32,2048]{1,0:T(8,128)S(1)} %copy-done, f32[32,2048]{1,0:T(8,128)S(1)} %copy-done.1, f32[32,2048]{1,0:T(8,128)S(1)} %copy-done.2, f32[32,2048]{1,0:T(8,128)S(1)} %copy-done.3, ...), custom_call_target="tpu_custom_call" | custom-call | tf_op jit(solution)/shard_map/route/pallas_call | solution.py:390
  30.6 11.0 %all_to_all.17 = f32[32,1,128]{2,1,0:T(1,128)S(1)} all-to-all(f32[32,1,128]{2,1,0:T(1,128)S(1)} %bitcast.12), channel_id=1, replica_groups=mesh['member'=8,'tile'=32] {'tile'}, dimensions={0} | all-to-all | bytes 32768 | tf_op jit(solution)/shard_map/all_to_all | solution.py:412
  41.6 1.0 %reach_sums.1 = f32[16,128]{1,0:T(8,128)} custom-call(f32[128,128]{1,0:T(8,128)S(1)} %bitcast.9, f32[32,128]{1,0:T(8,128)S(1)} %bitcast.11), custom_call_target="tpu_custom_call" | custom-call | tf_op jit(solution)/shard_map/reach_sums/pallas_call | solution.py:413
Async XLA Ops:
  0.6 23.4 %copy-start = (f32[32,2048]{1,0:T(8,128)S(1)}, f32[32,2048]{1,0:T(8,128)}, u32[]{:S(2)}) copy-start(f32[32,2048]{1,0:T(8,128)} %head_init.1) | copy-start | bytes 786436
  0.6 23.4 %copy-start.1 = (f32[32,2048]{1,0:T(8,128)S(1)}, f32[32,2048]{1,0:T(8,128)}, u32[]{:S(2)}) copy-start(f32[32,2048]{1,0:T(8,128)} %sub_init.1) | copy-start | bytes 786436
  0.7 23.4 %copy-start.2 = (f32[32,2048]{1,0:T(8,128)S(1)}, f32[32,2048]{1,0:T(8,128)}, u32[]{:S(2)}) copy-start(f32[32,2048]{1,0:T(8,128)} %conduct.3) | copy-start | bytes 786436
  0.7 23.4 %copy-start.3 = (f32[32,2048]{1,0:T(8,128)S(1)}, f32[32,2048]{1,0:T(8,128)}, u32[]{:S(2)}) copy-start(f32[32,2048]{1,0:T(8,128)} %drain.3) | copy-start | bytes 786436
  0.7 23.4 %copy-start.4 = (s32[32,2048]{1,0:T(8,128)S(1)}, s32[32,2048]{1,0:T(8,128)}, u32[]{:S(2)}) copy-start(s32[32,2048]{1,0:T(8,128)} %code.3) | copy-start | bytes 786436
  2.1 21.9 %collective-permute-start = (f32[40,2048]{1,0:T(8,128)S(1)}, f32[40,2048]{1,0:T(8,128)S(1)}, u32[]{:S(2)}, u32[]{:S(2)}) collective-permute-start(f32[40,2048]{1,0:T(8,128)S(1)} %get-tuple-element.12), channel_id=1, source_target_pairs={{0,1},{1,0},{2,3},{3,2},{4,5},{5,4},{6,7},{7,6},{8,9},{9,8},{10,11... | collective-permute-start | bytes 983048 | tf_op jit(solution)/shard_map/ppermute | solution.py:382
  5.4 18.6 %collective-permute-start.1 = (f32[40,2048]{1,0:T(8,128)S(1)}, f32[40,2048]{1,0:T(8,128)S(1)}, u32[]{:S(2)}, u32[]{:S(2)}) collective-permute-start(f32[40,2048]{1,0:T(8,128)S(1)} %get-tuple-element.13), channel_id=1, source_target_pairs={{1,2},{2,1},{3,4},{4,3},{5,6},{6,5},{7,8},{8,7},{9,10},{10,9},{11,... | collective-permute-start | bytes 983048 | tf_op jit(solution)/shard_map/ppermute | solution.py:383
